TPU v7x, 256 devices: a whole 4x4x8 slice. The times are simulated.
256 devices in a mesh: grp: 2 (over x_hi), rows: 64 (over y, z, core), cols: 2 (over x_lo).
Axes of the slice: x: 4 (x_hi: 2, x_lo: 2; x = x_hi * 2 + x_lo), y: 4, z: 8, core: 2. Of those that a mesh axis runs over, the one named last changes fastest.
Arguments:
- band_vectors: float32 [49152, 1024], P('rows'), may hold values from -6 to 6
- coulomb: float32 [49152], P('rows'), may hold values from 0.1 to 10
- pair_weight: float32 [1536], replicated, may hold values from 0.25 to 4
- occ_index: int32 [1536], replicated, may hold values from 0 to 255
- vir_index: int32 [1536], replicated, may hold values from 256 to 1023
- freq_index: int32 [1024], replicated, may hold values from 0 to 15
- freq_table: float32 [16], replicated, may hold values from 0.3 to 3
Outputs:
- self_energy: float32 [1024, 1024], P(('rows', 'cols'), 'grp')
Inputs may be any that keep to these rules, and one draw needn't show every extreme that they name: `occ_index`: every pair's occupied band lies below 256. `vir_index`: every pair's empty band lies at 256 or above.
All inputs are finite; a program needn't handle non-finite values.
Results may differ from a plain program's by a relative error of at most 0.0001.
Values sent between devices are 32-bit elements; how exact they have to be, the bound alone decides.
A program may use at most 64 MiB of HBM per device.

v0:
```python
import math

import jax
import jax.numpy as jnp
from jax import lax
from jax.sharding import Mesh
from jax.sharding import PartitionSpec as P

NB = 49152
PANEL = 512
ROWS = ("rows_0", "rows_1", "rows_2")
ROWS_COLS = ("rows_0", "rows_1", "rows_2", "cols")


def padded_to(lines, count):
    spare = -lines.shape[0] % count
    if not spare:
        return lines
    return jnp.concatenate([lines, jnp.zeros((spare, *lines.shape[1:]), lines.dtype)])


def sent_to_all(value, axis):
    copies = jnp.broadcast_to(value, (lax.axis_size(axis), *value.shape))
    return lax.all_to_all(copies, axis, split_axis=0, concat_axis=0, tiled=True)


def joined_along(tiles, dim):
    dims = list(tiles.shape[1:])
    dims[dim] *= tiles.shape[0]
    return jnp.moveaxis(tiles, 0, dim).reshape(dims)


def gather_axes(value, axes, dim):
    far, near = axes
    tiles = sent_to_all(sent_to_all(value, far), near)
    return joined_along(tiles.swapaxes(0, 1).reshape(-1, *value.shape), dim)


def cut_along(value, dim, count):
    before, after = (value.shape[:dim], value.shape[dim + 1 :])
    return jnp.moveaxis(value.reshape(*before, count, -1, *after), dim, 0)


def sum_at_owner(value, axis, dim):
    tiles = cut_along(value, dim, lax.axis_size(axis))
    arrived = lax.all_to_all(tiles, axis, split_axis=0, concat_axis=0, tiled=True)
    return arrived.sum(axis=0)


def sum_in_two_steps(value, axes, dim):
    far, near = axes
    tiles = cut_along(value, dim, lax.axis_size(far))
    nearer = sum_at_owner(tiles, near, dim + 1)
    arrived = lax.all_to_all(nearer, far, split_axis=0, concat_axis=0, tiled=True)
    return arrived.sum(axis=0)


def nested_sum(value, axes):
    lines = value.reshape(-1, value.shape[-1])
    padded = padded_to(lines, lax.axis_size(axes[0]) * lax.axis_size(axes[1]))
    whole = gather_axes(sum_in_two_steps(padded, axes, 0), axes, 0)
    return lax.slice_in_dim(whole, 0, len(lines)).reshape(value.shape)


def collect(value, axis, dim):
    tiles = sent_to_all(value, axis)
    return joined_along(tiles, dim)


def per_device(band_vectors, coulomb, pair_weight, occ_index, vir_index, freq_index, freq_table):
    highest = lax.Precision.HIGHEST
    row_count = lax.axis_size(ROWS)
    col_count = lax.axis_size("cols")
    group_count = lax.axis_size("grp")
    column = lax.axis_index("cols")
    group = lax.axis_index("grp")
    basis_rows = band_vectors.shape[0]
    band_total = band_vectors.shape[1]
    pair_cols = (
        jnp.take(band_vectors, occ_index, axis=1)
        * jnp.take(band_vectors, vir_index, axis=1)
        * pair_weight[None, :]
    )
    table_size = freq_table.shape[0]
    matches = freq_index[:, None] == jnp.arange(table_size, dtype=jnp.int32)[None, :]
    band_weight = jnp.sum(jnp.where(matches, freq_table[None, :], 0.0), axis=1)
    quarter = PANEL // col_count
    panel_start = group * PANEL + column * quarter
    weighted = lax.dynamic_slice_in_dim(pair_cols, panel_start, quarter, 1) * coulomb[:, None]
    partial_response = lax.dot_general(
        pair_cols,
        weighted,
        (((0,), (0,)), ((), ())),
        precision=highest,
        preferred_element_type=jnp.float32,
    )
    response = nested_sum(partial_response, (("rows_0", "rows_1"), "rows_2")) * (1.0 / NB)
    band_rows = band_total // (row_count * col_count)
    half_rows = band_rows // group_count
    shaped = band_vectors.reshape(basis_rows, row_count, col_count, group_count, half_rows)
    chosen = lax.dynamic_index_in_dim(shaped, column, 2, keepdims=False)
    chosen = lax.dynamic_index_in_dim(chosen, group, 2, keepdims=False).reshape(
        basis_rows, row_count * half_rows
    )
    shaped_weight = band_weight.reshape(row_count, col_count, group_count, half_rows)
    chosen_weight = lax.dynamic_index_in_dim(shaped_weight, column, 1, keepdims=False)
    chosen_weight = lax.dynamic_index_in_dim(chosen_weight, group, 1, keepdims=False).reshape(
        row_count * half_rows
    )
    band_cols = chosen * coulomb[:, None] * chosen_weight[None, :]
    own_half = sum_in_two_steps(
        lax.dot_general(
            band_cols,
            pair_cols,
            (((0,), (0,)), ((), ())),
            precision=highest,
            preferred_element_type=jnp.float32,
        ),
        (("rows_0", "rows_1"), "rows_2"),
        0,
    ) * (1.0 / math.sqrt(NB))
    coupling = collect(own_half, "grp", 0)
    neighbour_coupling = collect(coupling, "cols", 0)
    partial_mixed = jnp.dot(
        neighbour_coupling, response, precision=highest, preferred_element_type=jnp.float32
    )
    mixed_rows = lax.all_to_all(partial_mixed, "cols", split_axis=0, concat_axis=1, tiled=True)
    own_panel = lax.dynamic_slice_in_dim(coupling, group * PANEL, PANEL, 1)
    partial_energy = lax.dot_general(
        mixed_rows,
        gather_axes(own_panel, (("rows_0", "rows_1"), ("rows_2", "cols")), 0),
        (((1,), (1,)), ((), ())),
        precision=highest,
        preferred_element_type=jnp.float32,
    )
    scale = 1.0 / math.sqrt(PANEL * group_count)
    return sum_at_owner(partial_energy * scale, "grp", 1)


def solution(mesh):
    torus = Mesh(
        mesh.devices.reshape(mesh.shape["grp"], 4, 8, 2, mesh.shape["cols"]),
        ("grp", "rows_0", "rows_1", "rows_2", "cols"),
    )
    placed = (P(ROWS, None), P(ROWS), P(), P(), P(), P(), P())
    return jax.shard_map(
        per_device, mesh=torus, in_specs=placed, out_specs=P(ROWS_COLS, "grp"), check_vma=False
    )
```

profile of v0, /device:TPU:1, one launch (start us, length us, event | category | flops | bytes accessed | tf_op | source)
XLA Modules:
  0.0 222.8 jit_solution(17553575773614387339)
XLA Ops:
  6.6 5.5 %gather_fusion.1 = f32[1536,768]{1,0:T(8,128)} fusion(f32[768,1024]{0,1:T(8,128)S(1)} %copy.35, s32[2048]{0:T(1024)S(1)} %pad_clamp_fusion), kind=kCustom, calls=%fused_computation.1.clone | custom fusion | bytes 9443328 | tf_op jit(solution)/shard_map/jit(_take)/gather | solution.py:81
  12.2 5.6 %gather_fusion = f32[1536,768]{1,0:T(8,128)} fusion(f32[768,1024]{0,1:T(8,128)S(1)} %copy.35, s32[2048]{0:T(1024)S(1)} %pad_clamp_fusion.1), kind=kCustom, calls=%fused_computation.clone | custom fusion | bytes 9443328 | tf_op jit(solution)/shard_map/jit(_take)/gather | solution.py:80
  20.3 4.4 %fusion.2 = f32[768,1536]{0,1:T(8,128)S(1)} fusion(f32[1536,768]{1,0:T(8,128)} %gather_fusion.1, f32[1536,768]{1,0:T(8,128)} %gather_fusion, f32[1536]{0:T(1024)S(1)} %copy-done.2, pred[1536]{0:T(1024)(128)(4,1)S(1)} %get-tuple-element.6, pred[1536]{0:T(1024)(128)(4,1)S(1)} %get-tuple-element.7), kind=kLoop, calls=%fused_computation.5 | loop fusion | flops 4718592 | bytes 14164992 | tf_op jit(solution)/shard_map/mul | solution.py:80
  24.7 4.4 %fusion.3 = f32[2,32,4,1536]{3,1,2,0:T(8,128)S(1)} fusion(f32[768,1536]{0,1:T(8,128)S(1)} %fusion.2, f32[32,2,4,768]{3,2,1,0:T(4,128)S(1)} %dot_general.17), kind=kOutput, calls=%fused_computation.6 | convolution fusion | flops 3623878656 | bytes 7077888 | tf_op jit(solution)/shard_map/dot_general | solution.py:112
  29.1 7.8 %all_to_all.71 = f32[2,32,4,1536]{3,1,2,0:T(8,128)S(1)} all-to-all(f32[2,32,4,1536]{3,1,2,0:T(8,128)S(1)} %fusion.3), channel_id=1, replica_groups=mesh['grp'=2,'rows_0'=4,'rows_1'=8,'rows_2'=2,'cols'=2] {'rows_2'}, dimensions={0} | all-to-all | bytes 3145728 | tf_op jit(solution)/shard_map/all_to_all | solution.py:46
  38.5 9.5 %all-to-all-start.1 = ((f32[32,4,1536]{2,1,0:T(4,128)}), f32[32,4,1536]{2,1,0:T(4,128)S(1)}, u32[]{:S(2)}, u32[]{:S(2)}) async-start(f32[32,4,1536]{2,1,0:T(4,128)} %copy.40), calls=%async_computation.1 | async-start | bytes 1572864 | tf_op jit(solution)/shard_map/all_to_all | solution.py:54
  48.0 6.5 %fusion.7 = f32[1536,256]{1,0:T(8,128)S(1)} fusion(f32[768,1536]{0,1:T(8,128)} %copy-done, s32[]{:T(128)S(6)} %select_n.38, f32[768]{0:T(1024)S(1)} %copy-done.1), kind=kOutput, calls=%fused_computation.11 | convolution fusion | flops 3624075264 | bytes 7080964 | tf_op jit(solution)/shard_map/dot_general | solution.py:90
  55.8 11.0 %all-to-all-done.1 = f32[32,4,1536]{2,1,0:T(4,128)S(1)} async-done(((f32[32,4,1536]{2,1,0:T(4,128)}), f32[32,4,1536]{2,1,0:T(4,128)S(1)}, u32[]{:S(2)}, u32[]{:S(2)}) %all-to-all-start.1) | async-done | bytes 786464 | tf_op jit(solution)/shard_map/all_to_all | solution.py:54
  66.8 8.3 %all-to-all-start.4 = ((f32[2,32,24,256]{3,2,1,0:T(8,128)}), f32[2,32,24,256]{3,2,1,0:T(8,128)S(1)}, u32[]{:S(2)}, u32[]{:S(2)}) async-start(f32[2,32,24,256]{3,2,1,0:T(8,128)} %bitcast.41), calls=%async_computation.4 | async-start | bytes 3145728 | tf_op jit(solution)/shard_map/all_to_all | solution.py:46
  78.0 4.0 %all-to-all-start.2 = ((f32[2,4,1536]{2,1,0:T(4,128)}), f32[2,4,1536]{2,1,0:T(4,128)S(1)}, u32[]{:S(2)}, u32[]{:S(2)}) async-start(f32[2,4,1536]{2,1,0:T(4,128)} %broadcast_in_dim.47), calls=%async_computation.2 | async-start | bytes 98304 | tf_op jit(solution)/shard_map/all_to_all | solution.py:24
  83.0 3.3 %all-to-all-done.2 = f32[2,4,1536]{2,1,0:T(4,128)S(1)} async-done(((f32[2,4,1536]{2,1,0:T(4,128)}), f32[2,4,1536]{2,1,0:T(4,128)S(1)}, u32[]{:S(2)}, u32[]{:S(2)}) %all-to-all-start.2) | async-done | bytes 49184 | tf_op jit(solution)/shard_map/all_to_all | solution.py:24
  86.4 5.3 %all-to-all-start.5 = ((f32[32,24,256]{2,1,0:T(8,128)}), f32[32,24,256]{2,1,0:T(8,128)S(1)}, u32[]{:S(2)}, u32[]{:S(2)}) async-start(f32[32,24,256]{2,1,0:T(8,128)} %reduce_sum.57), calls=%async_computation.5 | async-start | bytes 1572864 | tf_op jit(solution)/shard_map/all_to_all | solution.py:54
  91.7 18.8 %all-to-all-done.5 = f32[32,24,256]{2,1,0:T(8,128)S(1)} async-done(((f32[32,24,256]{2,1,0:T(8,128)}), f32[32,24,256]{2,1,0:T(8,128)S(1)}, u32[]{:S(2)}, u32[]{:S(2)}) %all-to-all-start.5) | async-done | bytes 786464 | tf_op jit(solution)/shard_map/all_to_all | solution.py:54
  111.1 3.3 %all-to-all-start.3 = ((f32[2,8,1536]{2,1,0:T(8,128)}), f32[2,8,1536]{2,1,0:T(8,128)S(1)}, u32[]{:S(2)}, u32[]{:S(2)}) async-start(f32[2,8,1536]{2,1,0:T(8,128)} %broadcast_in_dim.48), calls=%async_computation.3 | async-start | bytes 196608 | tf_op jit(solution)/shard_map/all_to_all | solution.py:24
  114.5 3.1 %all-to-all-done.3 = f32[2,8,1536]{2,1,0:T(8,128)S(1)} async-done(((f32[2,8,1536]{2,1,0:T(8,128)}), f32[2,8,1536]{2,1,0:T(8,128)S(1)}, u32[]{:S(2)}, u32[]{:S(2)}) %all-to-all-start.3) | async-done | bytes 98336 | tf_op jit(solution)/shard_map/all_to_all | solution.py:24
  118.4 8.2 %all-to-all-start.9 = ((f32[32,8,512]{2,1,0:T(8,128)}), f32[32,8,512]{2,1,0:T(8,128)S(1)}, u32[]{:S(2)}, u32[]{:S(2)}) async-start(f32[32,8,512]{2,1,0:T(8,128)} %broadcast_in_dim.51), calls=%async_computation.9 | async-start | bytes 1048576 | tf_op jit(solution)/shard_map/all_to_all | solution.py:24
  126.7 11.8 %all-to-all-done.9 = f32[32,8,512]{2,1,0:T(8,128)S(1)} async-done(((f32[32,8,512]{2,1,0:T(8,128)}), f32[32,8,512]{2,1,0:T(8,128)S(1)}, u32[]{:S(2)}, u32[]{:S(2)}) %all-to-all-start.9) | async-done | bytes 524320 | tf_op jit(solution)/shard_map/all_to_all | solution.py:24
  138.6 24.2 %all_to_all.72 = f32[32,24,256]{2,1,0:T(8,128)S(1)} all-to-all(f32[32,24,256]{2,1,0:T(8,128)S(1)} %broadcast_in_dim.49), channel_id=1, replica_groups=mesh['grp'=2,'rows_0'=4,'rows_1'=8,'rows_2'=2,'cols'=2] {'rows_0','rows_1'}, dimensions={0} | all-to-all | bytes 1572864 | tf_op jit(solution)/shard_map/all_to_all | solution.py:24
  163.0 13.0 %all_to_all.73 = f32[2,32,24,256]{3,2,1,0:T(8,128)} all-to-all(f32[2,32,24,256]{3,2,1,0:T(8,128)S(1)} %broadcast_in_dim.50), channel_id=1, replica_groups=mesh['grp'=2,'rows_0'=4,'rows_1'=8,'rows_2'=2,'cols'=2] {'rows_2'}, dimensions={0} | all-to-all | bytes 3145728 | tf_op jit(solution)/shard_map/all_to_all | solution.py:24
  177.6 3.9 %all-to-all-start.10 = ((f32[4,32,8,512]{3,2,1,0:T(8,128)}), f32[4,32,8,512]{3,2,1,0:T(8,128)S(1)}, u32[]{:S(2)}, u32[]{:S(2)}) async-start(f32[4,32,8,512]{3,2,1,0:T(8,128)} %broadcast_in_dim.52), calls=%async_computation.10 | async-start | bytes 4194304 | tf_op jit(solution)/shard_map/all_to_all | solution.py:24
  184.6 21.6 %all-to-all-done.10 = f32[4,32,8,512]{3,2,1,0:T(8,128)S(1)} async-done(((f32[4,32,8,512]{3,2,1,0:T(8,128)}), f32[4,32,8,512]{3,2,1,0:T(8,128)S(1)}, u32[]{:S(2)}, u32[]{:S(2)}) %all-to-all-start.10) | async-done | bytes 2097184 | tf_op jit(solution)/shard_map/all_to_all | solution.py:24
  206.2 3.2 %all-to-all-start.8 = ((f32[2,8,256]{2,1,0:T(8,128)}), f32[2,8,256]{2,1,0:T(8,128)S(1)}, u32[]{:S(2)}, u32[]{:S(2)}) async-start(f32[2,8,256]{2,1,0:T(8,128)} %fusion.12), calls=%async_computation.8 | async-start | bytes 32768 | tf_op jit(solution)/shard_map/all_to_all | solution.py:127
  212.2 3.4 %convolution_multiply_fusion = f32[8,1024]{1,0:T(8,128)S(1)} fusion(f32[8,512]{1,0:T(8,128)S(1)} %bitcast.46, f32[1024,512]{1,0:T(8,128)} %bitcast.42), kind=kOutput, calls=%fused_computation.9 | convolution fusion | flops 50339840 | bytes 2146304 | tf_op jit(solution)/shard_map/dot_general | solution.py:129
  215.5 6.7 %all_to_all.74 = f32[2,8,512]{2,1,0:T(8,128)S(1)} all-to-all(f32[2,8,512]{2,1,0:T(8,128)S(1)} %bitcast.45), channel_id=1, replica_groups=mesh['grp'=2,'rows_0'=4,'rows_1'=8,'rows_2'=2,'cols'=2] {'grp'}, dimensions={0} | all-to-all | bytes 65536 | tf_op jit(solution)/shard_map/all_to_all | solution.py:46
  (47 shorter events, 25.4 us)
Async XLA Ops:
  17.8 1.5 copy-start.3
  17.8 1.5 copy-start.4
  17.8 2.1 copy-start.1
  17.8 2.5 %copy-start.2 = (f32[1536]{0:T(1024)S(1)}, f32[1536]{0:T(1024)}, u32[]{:S(2)}) copy-start(f32[1536]{0:T(1024)} %param.11) | copy-start | bytes 18436
  24.7 4.4 %copy-start = (f32[768,1536]{0,1:T(8,128)}, f32[768,1536]{0,1:T(8,128)S(1)}, u32[]{:S(2)}) copy-start(f32[768,1536]{0,1:T(8,128)S(1)} %fusion.2) | copy-start | bytes 14155780
  38.5 28.3 %all-to-all-start.1 = ((f32[32,4,1536]{2,1,0:T(4,128)}), f32[32,4,1536]{2,1,0:T(4,128)S(1)}, u32[]{:S(2)}, u32[]{:S(2)}) async-start(f32[32,4,1536]{2,1,0:T(4,128)} %copy.40), calls=%async_computation.1 | async-start | bytes 1572864 | tf_op jit(solution)/shard_map/all_to_all | solution.py:54
  66.8 10.5 %all-to-all-start.4 = ((f32[2,32,24,256]{3,2,1,0:T(8,128)}), f32[2,32,24,256]{3,2,1,0:T(8,128)S(1)}, u32[]{:S(2)}, u32[]{:S(2)}) async-start(f32[2,32,24,256]{3,2,1,0:T(8,128)} %bitcast.41), calls=%async_computation.4 | async-start | bytes 3145728 | tf_op jit(solution)/shard_map/all_to_all | solution.py:46
  78.0 8.4 %all-to-all-start.2 = ((f32[2,4,1536]{2,1,0:T(4,128)}), f32[2,4,1536]{2,1,0:T(4,128)S(1)}, u32[]{:S(2)}, u32[]{:S(2)}) async-start(f32[2,4,1536]{2,1,0:T(4,128)} %broadcast_in_dim.47), calls=%async_computation.2 | async-start | bytes 98304 | tf_op jit(solution)/shard_map/all_to_all | solution.py:24
  86.4 24.1 %all-to-all-start.5 = ((f32[32,24,256]{2,1,0:T(8,128)}), f32[32,24,256]{2,1,0:T(8,128)S(1)}, u32[]{:S(2)}, u32[]{:S(2)}) async-start(f32[32,24,256]{2,1,0:T(8,128)} %reduce_sum.57), calls=%async_computation.5 | async-start | bytes 1572864 | tf_op jit(solution)/shard_map/all_to_all | solution.py:54
  111.1 6.5 %all-to-all-start.3 = ((f32[2,8,1536]{2,1,0:T(8,128)}), f32[2,8,1536]{2,1,0:T(8,128)S(1)}, u32[]{:S(2)}, u32[]{:S(2)}) async-start(f32[2,8,1536]{2,1,0:T(8,128)} %broadcast_in_dim.48), calls=%async_computation.3 | async-start | bytes 196608 | tf_op jit(solution)/shard_map/all_to_all | solution.py:24
  118.4 20.1 %all-to-all-start.9 = ((f32[32,8,512]{2,1,0:T(8,128)}), f32[32,8,512]{2,1,0:T(8,128)S(1)}, u32[]{:S(2)}, u32[]{:S(2)}) async-start(f32[32,8,512]{2,1,0:T(8,128)} %broadcast_in_dim.51), calls=%async_computation.9 | async-start | bytes 1048576 | tf_op jit(solution)/shard_map/all_to_all | solution.py:24
  177.6 28.7 %all-to-all-start.10 = ((f32[4,32,8,512]{3,2,1,0:T(8,128)}), f32[4,32,8,512]{3,2,1,0:T(8,128)S(1)}, u32[]{:S(2)}, u32[]{:S(2)}) async-start(f32[4,32,8,512]{3,2,1,0:T(8,128)} %broadcast_in_dim.52), calls=%async_computation.10 | async-start | bytes 4194304 | tf_op jit(solution)/shard_map/all_to_all | solution.py:24
  206.2 5.9 %all-to-all-start.8 = ((f32[2,8,256]{2,1,0:T(8,128)}), f32[2,8,256]{2,1,0:T(8,128)S(1)}, u32[]{:S(2)}, u32[]{:S(2)}) async-start(f32[2,8,256]{2,1,0:T(8,128)} %fusion.12), calls=%async_computation.8 | async-start | bytes 32768 | tf_op jit(solution)/shard_map/all_to_all | solution.py:127
where the time goes:
time: 226 us; the launch traced here: 223 us
  waiting for transfers between devices  72.8 us (32%)
  blocking collectives  51.7 us (23%)
  starting transfers between devices  45.9 us (20%)
  local copies, waits for them, and re-layouts  26.2 us (12%)
  matrix products  15.6 us (7%)
  other arithmetic  10.3 us (5%)
    all_to_all x4, waiting for transfers between devices, sent_to_all(): return lax.all_to_all(copies, axis, split_axis=0, concat_axis=0, tiled=True)  39.9 us
    all_to_all x2, blocking collectives, sent_to_all(): return lax.all_to_all(copies, axis, split_axis=0, concat_axis=0, tiled=True)  37.2 us
    all_to_all x2, waiting for transfers between devices, sum_in_two_steps(): lax.all_to_all(nearer, far, split_axis=0, concat_axis=0, tiled=True)  29.8 us
    all_to_all x4, starting transfers between devices, sent_to_all(): return lax.all_to_all(copies, axis, split_axis=0, concat_axis=0, tiled=True)  19.5 us
    all_to_all x2, starting transfers between devices, sum_in_two_steps(): lax.all_to_all(nearer, far, split_axis=0, concat_axis=0, tiled=True)  14.8 us
    all_to_all x2, blocking collectives, sum_at_owner(): lax.all_to_all(tiles, axis, split_axis=0, concat_axis=0, tiled=True)  14.5 us
    all_to_all x1, starting transfers between devices, sum_at_owner(): lax.all_to_all(tiles, axis, split_axis=0, concat_axis=0, tiled=True)  8.35 us
    dot_general x1, matrix products, per_device(): lax.dot_general(pair_cols, weighted, (((0,), (0,)), ((), ())), precision=...  6.53 us
  transfers between devices with their start and end apart: 8, of which 8 were waited for; matrix products, arithmetic and copies ran while one was open for 6% of the time, Pallas kernels for 0%

commit v1 on v0

v1 whole, which is shorter than its diff:
```python
import functools
import math

import jax
import jax.numpy as jnp
from jax import lax
from jax.experimental import pallas as pl
from jax.experimental.pallas import tpu as pltpu
from jax.sharding import Mesh
from jax.sharding import PartitionSpec as P

NB = 49152
ROWS = ("rows_0", "rows_1", "rows_2")
ROWS_COLS = ("rows_0", "rows_1", "rows_2", "cols")
MESH = pl.DeviceIdType.MESH
F32 = jnp.float32
BF16 = jnp.bfloat16
KB = 768
NK = KB // 128
HALF = 768


def split(x):
    hi = x.astype(BF16)
    return hi, (x - hi.astype(F32)).astype(BF16)


def pair_kernel(occ, vir, weight, v_ref, c_ref, pt_hi, pt_lo, w_hi, w_lo, vt, pt, wn):
    plane = lax.axis_index("grp") * 2 + lax.axis_index("cols")
    for k in range(NK):
        for nb in range(8):
            block = v_ref[k * 128 : (k + 1) * 128, nb * 128 : (nb + 1) * 128]
            vt[pl.ds(nb * 1024 + k, 128, stride=8), :] = block.T

    for half in range(2):
        for b in range(6):

            def one(i, carry, half=half, b=b):
                for u in range(8):
                    at = i * 8 + u
                    p = 256 * b + 128 * half + at
                    o = pl.multiple_of(occ[p] * 8, 8)
                    v = pl.multiple_of(vir[p] * 8, 8)
                    to = pl.multiple_of((768 * half + 128 * b + at) * 8, 8)
                    pt[pl.ds(to, 8), :] = vt[pl.ds(o, 8), :] * vt[pl.ds(v, 8), :] * weight[p]
                return carry

            lax.fori_loop(0, 16, one, 0)

    def rows(b, carry):
        base = pl.multiple_of(b * 128, 128)
        for k in range(NK):
            x = pt[pl.ds(base * 8 + k, 128, stride=8), :]
            hi, lo = split(x)
            pt_hi[pl.ds(base, 128), k * 128 : (k + 1) * 128] = hi
            pt_lo[pl.ds(base, 128), k * 128 : (k + 1) * 128] = lo
        return carry

    lax.fori_loop(0, 12, rows, 0)
    for k in range(NK):
        cols = slice(k * 128, (k + 1) * 128)
        c = c_ref[0:1, cols]
        for half in range(2):
            x = pt[pl.ds((768 * half + 128 * plane) * 8 + k, 128, stride=8), :] * c
            hi, lo = split(x)
            w_hi[half * 128 : (half + 1) * 128, cols] = hi
            w_lo[half * 128 : (half + 1) * 128, cols] = lo
        for g in range(32):
            wn[g * 8 : (g + 1) * 8, :] = vt[pl.ds((32 * g + 8 * plane) * 8 + k, 8, stride=8), :] * c
        hi, lo = split(wn[...])
        w_hi[256:512, cols] = hi
        w_lo[256:512, cols] = lo


def nt(a, b):
    return lax.dot_general(a, b, (((1,), (1,)), ((), ())), preferred_element_type=F32)


def nn(a, b):
    return lax.dot_general(a, b, (((1,), (0,)), ((), ())), preferred_element_type=F32)


def main_kernel(
    pt_hi, pt_lo, w_hi, w_lo, fidx, ftab, out_ref,
    r_oth, x_oth, r_in, x_in, r_acc, x_acc,
    zin_m, zin_p, yin_m, yin_p, ry_in, xz_in,
    x32, rfull, yfull, mbuf, m_in, sbuf, s_in,
    send, recv,
):
    y = lax.axis_index("rows_0")
    z = lax.axis_index("rows_1")
    c = lax.axis_index("rows_2")
    g = lax.axis_index("grp")
    cl = lax.axis_index("cols")
    plane = 2 * g + cl
    started = []
    count = [0]

    def copy(src, dst, to):
        i = count[0]
        count[0] += 1
        d = pltpu.make_async_remote_copy(
            src_ref=src, dst_ref=dst, send_sem=send.at[i], recv_sem=recv.at[i],
            device_id=to, device_id_type=MESH,
        )
        d.start()
        started.append(d)
        return d

    def zto(k):
        return {"rows_1": lax.rem(z + k + 8, 8)}

    def yto(k):
        return {"rows_0": lax.rem(y + k + 4, 4)}

    def xto(rel):
        rg, rc, rl = rel
        return {
            "grp": lax.rem(g + rg, 2),
            "rows_2": lax.rem(c + rc, 2),
            "cols": lax.rem(cl + rl, 2),
        }

    rels = [(a, b, d) for a in range(2) for b in range(2) for d in range(2)][1:]

    barrier = pltpu.get_barrier_semaphore()
    for k in range(1, 8):
        pl.semaphore_signal(barrier, inc=1, device_id=zto(k), device_id_type=MESH)
    for k in range(1, 4):
        pl.semaphore_signal(barrier, inc=1, device_id=yto(k), device_id_type=MESH)
    for rel in rels:
        pl.semaphore_signal(barrier, inc=1, device_id=xto(rel), device_id_type=MESH)

    def products(half, r_out, x_out):
        base = pl.multiple_of(half * HALF, HALF)
        ph = pt_hi[pl.ds(base, HALF), :]
        pw = pt_lo[pl.ds(base, HALF), :]
        qh, ql = w_hi[0:256, :], w_lo[0:256, :]
        r_out[...] = nt(ph, qh) + nt(ph, ql) + nt(pw, qh)
        for b in range(3):
            at = pl.multiple_of(half * HALF + b * 256, 256)
            bh = pt_hi[pl.ds(at, 256), :]
            bl = pt_lo[pl.ds(at, 256), :]
            nh, nl = w_hi[256:512, :], w_lo[256:512, :]
            x_out[:, b * 256 : (b + 1) * 256] = nt(nh, bh) + nt(nl, bh) + nt(nh, bl)

    products(1 - c, r_oth, x_oth)
    pl.semaphore_wait(barrier, 17)
    core = {"rows_2": 1 - c}
    dr = copy(r_oth, r_in, core)
    dx = copy(x_oth, x_in, core)
    products(c, r_acc, x_acc)
    dr.wait_recv()
    r_acc[...] += r_in[...]

    def zrows(k, start=0, size=96):
        return pl.ds(pl.multiple_of(lax.rem(z + k + 8, 8) * 96 + start, 8), size)

    def yrows(k, start=0, size=64):
        return pl.ds(pl.multiple_of(lax.rem(y + k + 4, 4) * 64 + start, 8), size)

    zm = copy(r_acc.at[zrows(4, 0, 48)], zin_m.at[0, 0:48], zto(-1))
    zp = copy(r_acc.at[zrows(4, 48, 48)], zin_p.at[0, 48:96], zto(1))
    dx.wait_recv()
    x_acc[...] += x_in[...]
    ym = copy(x_acc.at[yrows(2, 0, 32)], yin_m.at[0, 0:32], yto(-1))
    yp = copy(x_acc.at[yrows(2, 32, 32)], yin_p.at[0, 32:64], yto(1))

    def zstep(s, zm, zp):
        zm.wait_recv()
        if s == 1:
            zin_m[0, 0:48] += r_acc[zrows(-3, 0, 48)]
            zin_m[0, 48:96] = r_acc[zrows(-3, 48, 48)]
        else:
            zin_m[s - 1] += r_acc[zrows(s - 4)]
        zm = copy(zin_m.at[s - 1], zin_m.at[s], zto(-1))
        zp.wait_recv()
        if s == 1:
            zin_p[0, 48:96] += r_acc[zrows(3, 48, 48)]
            zin_p[0, 0:48] = r_acc[zrows(3, 0, 48)]
        else:
            zin_p[s - 1] += r_acc[zrows(4 - s)]
        zp = copy(zin_p.at[s - 1], zin_p.at[s], zto(1))
        return zm, zp

    zm, zp = zstep(1, zm, zp)
    ym.wait_recv()
    yin_m[0, 0:32] += x_acc[yrows(-1, 0, 32)]
    yin_m[0, 32:64] = x_acc[yrows(-1, 32, 32)]
    ym = copy(yin_m.at[0], yin_m.at[1], yto(-1))
    yp.wait_recv()
    yin_p[0, 32:64] += x_acc[yrows(1, 32, 32)]
    yin_p[0, 0:32] = x_acc[yrows(1, 0, 32)]
    yp = copy(yin_p.at[0], yin_p.at[1], yto(1))
    zm, zp = zstep(2, zm, zp)

    ym.wait_recv()
    yp.wait_recv()
    yin_m[1] += x_acc[yrows(0)] + yin_p[1]
    xz = []
    for k in (4, 3, 5, 2, 6, 1, 7):
        rows = pl.ds(pl.multiple_of(lax.rem(z + k, 8) * 8, 8), 8)
        xz.append(copy(yin_m.at[1, rows], xz_in.at[k], zto(k)))
    zm, zp = zstep(3, zm, zp)
    zm.wait_recv()
    zp.wait_recv()
    zin_m[3] += r_acc[zrows(0)] + zin_p[3]
    ry = []
    for k in (2, 1, 3):
        rows = pl.ds(pl.multiple_of(lax.rem(y + k, 4) * 24, 8), 24)
        ry.append(copy(zin_m.at[3, rows], ry_in.at[k], yto(k)))

    for d in xz:
        d.wait_recv()
    tile = yin_m[1, pl.ds(pl.multiple_of(z * 8, 8), 8)]
    for k in range(1, 8):
        tile = tile + xz_in[k]
    chip = y * 8 + z
    row = lax.broadcasted_iota(jnp.int32, (8, HALF), 0)
    factor = jnp.zeros((8, HALF), F32)
    for i in range(8):
        factor = jnp.where(row == i, ftab[fidx[32 * chip + 8 * plane + i]], factor)
    x32[plane] = tile * factor * (1.0 / math.sqrt(NB))
    xs = [copy(x32.at[plane], x32.at[plane], xto(rel)) for rel in ((1, 0, 0), (0, 0, 1), (1, 0, 1))]

    for d in ry:
        d.wait_recv()
    tile = zin_m[3, pl.ds(pl.multiple_of(y * 24, 8), 24)]
    for k in range(1, 4):
        tile = tile + ry_in[k]
    mine = pl.ds(pl.multiple_of((z * 4 + y) * 24, 8), 24)
    rfull[mine] = tile * (1.0 / NB)
    ry = [copy(rfull.at[mine], rfull.at[mine], yto(k)) for k in (2, 1, 3)]

    for d in xs:
        d.wait_recv()
    myrows = pl.multiple_of(chip * 32, 32)
    lanes = pl.ds(pl.multiple_of(plane * 128, 128), 128)
    for j in range(4):
        yfull[pl.ds(myrows + 8 * j, 8)] = x32[j, :, lanes]
    ymine = pl.ds(myrows, 32)
    yz = [copy(yfull.at[ymine], yfull.at[ymine], zto(k)) for k in (4, 3, 5, 2, 6, 1, 7)]

    for d in ry:
        d.wait_recv()

    def zfull(k, start=0, size=96):
        return rfull.at[zrows(k, start, size)]

    zm = copy(zfull(0), zfull(0), zto(-1))
    zp = copy(zfull(0), zfull(0), zto(1))
    for d in yz:
        d.wait_recv()

    def ychunk(k, start=0, size=256):
        return yfull.at[pl.ds(pl.multiple_of(lax.rem(y + k + 4, 4) * 256 + start, 8), size)]

    ym = copy(ychunk(0), ychunk(0), yto(-1))
    yp = copy(ychunk(0), ychunk(0), yto(1))
    for s in range(1, 3):
        zm.wait_recv()
        zm = copy(zfull(s), zfull(s), zto(-1))
        zp.wait_recv()
        zp = copy(zfull(-s), zfull(-s), zto(1))
        if s == 1:
            ym.wait_recv()
            ym = copy(ychunk(1, 0, 128), ychunk(1, 0, 128), yto(-1))
            yp.wait_recv()
            yp = copy(ychunk(-1, 128, 128), ychunk(-1, 128, 128), yto(1))
    zm.wait_recv()
    zm = copy(zfull(3, 0, 48), zfull(3, 0, 48), zto(-1))
    zp.wait_recv()
    zp = copy(zfull(-3, 48, 48), zfull(-3, 48, 48), zto(1))
    ym.wait_recv()
    yp.wait_recv()
    zm.wait_recv()
    zp.wait_recv()

    xh, xl = split(x32[...].reshape(32, HALF))
    rh, rl = split(rfull[...])
    m = nn(xh, rh) + nn(xl, rh) + nn(xh, rl)
    mbuf[0] = m[:, 0:128]
    mbuf[1] = m[:, 128:256]
    dm = copy(mbuf.at[1 - c], m_in, core)
    yh, yl = split(yfull[...])
    dm.wait_recv()
    mh, ml = split(mbuf[c] + m_in[...])
    s = nt(mh, yh) + nt(ml, yh) + nt(mh, yl)
    for tg in range(2):
        for tc in range(2):
            for tl in range(2):
                at = 16 * tc + 8 * tl
                sbuf[tg * 4 + tc * 2 + tl] = s[at : at + 8, tg * 512 : (tg + 1) * 512]
    ds = []
    for i, rel in enumerate(rels):
        to = xto(rel)
        t = to["grp"] * 4 + to["rows_2"] * 2 + to["cols"]
        ds.append(copy(sbuf.at[t], s_in.at[i], to))
    total = sbuf[g * 4 + c * 2 + cl]
    for i, d in enumerate(ds):
        d.wait_recv()
        total = total + s_in[i]
    out_ref[...] = total * (1.0 / math.sqrt(1024))
    for d in started:
        d.wait_send()


def per_device(band_vectors, coulomb, pair_weight, occ_index, vir_index, freq_index, freq_table):
    smem = pl.BlockSpec(memory_space=pltpu.SMEM)
    vmem = pl.BlockSpec(memory_space=pltpu.VMEM)
    pt_hi, pt_lo, w_hi, w_lo = pl.pallas_call(
        pair_kernel,
        out_shape=(
            jax.ShapeDtypeStruct((1536, KB), BF16),
            jax.ShapeDtypeStruct((1536, KB), BF16),
            jax.ShapeDtypeStruct((512, KB), BF16),
            jax.ShapeDtypeStruct((512, KB), BF16),
        ),
        in_specs=[smem, smem, smem, vmem, vmem],
        out_specs=(vmem, vmem, vmem, vmem),
        scratch_shapes=[
            pltpu.VMEM((8192, 128), F32),
            pltpu.VMEM((1536 * 8, 128), F32),
            pltpu.VMEM((256, 128), F32),
        ],
        name="pairs",
    )(occ_index, vir_index, pair_weight, band_vectors, coulomb.reshape(1, KB))
    return pl.pallas_call(
        main_kernel,
        out_shape=jax.ShapeDtypeStruct((8, 512), F32),
        in_specs=[vmem, vmem, vmem, vmem, smem, smem],
        out_specs=vmem,
        scratch_shapes=[
            pltpu.VMEM((HALF, 256), F32),
            pltpu.VMEM((256, HALF), F32),
            pltpu.VMEM((HALF, 256), F32),
            pltpu.VMEM((256, HALF), F32),
            pltpu.VMEM((HALF, 256), F32),
            pltpu.VMEM((256, HALF), F32),
            pltpu.VMEM((4, 96, 256), F32),
            pltpu.VMEM((4, 96, 256), F32),
            pltpu.VMEM((2, 64, HALF), F32),
            pltpu.VMEM((2, 64, HALF), F32),
            pltpu.VMEM((4, 24, 256), F32),
            pltpu.VMEM((8, 8, HALF), F32),
            pltpu.VMEM((4, 8, HALF), F32),
            pltpu.VMEM((HALF, 256), F32),
            pltpu.VMEM((1024, 128), F32),
            pltpu.VMEM((2, 32, 128), F32),
            pltpu.VMEM((32, 128), F32),
            pltpu.VMEM((8, 8, 512), F32),
            pltpu.VMEM((7, 8, 512), F32),
            pltpu.SemaphoreType.DMA((64,)),
            pltpu.SemaphoreType.DMA((64,)),
        ],
        compiler_params=pltpu.CompilerParams(collective_id=0, has_side_effects=True),
        name="window",
    )(pt_hi, pt_lo, w_hi, w_lo, freq_index, freq_table)


def solution(mesh):
    torus = Mesh(
        mesh.devices.reshape(mesh.shape["grp"], 4, 8, 2, mesh.shape["cols"]),
        ("grp", "rows_0", "rows_1", "rows_2", "cols"),
    )
    placed = (P(ROWS, None), P(ROWS), P(), P(), P(), P(), P())
    return jax.shard_map(
        per_device, mesh=torus, in_specs=placed, out_specs=P(ROWS_COLS, "grp"), check_vma=False
    )
```

time: 226 us -> 80.9 us (0.36); the launches traced: 223 us -> 80.7 us
  Pallas kernels: 0 us -> 78.1 us
  waiting for transfers between devices: 72.8 us -> 0 us
  blocking collectives: 51.7 us -> 0 us
  starting transfers between devices: 45.9 us -> 0 us
  local copies, waits for them, and re-layouts: 26.2 us -> 2.59 us
  matrix products: 15.6 us -> 0 us
  other arithmetic: 10.3 us -> 0 us
    pallas_call x0 -> x2, Pallas kernels: none -> 78.1 us  [the longest x1 66.9 us: per_device(): pl.pallas_call(main_kernel, out_shape=jax.ShapeDtypeStruct((8, 512), F32)...]
    all_to_all x8 -> x0, waiting for transfers between devices: 72.8 us -> none  [the longest x4 39.9 us: sent_to_all(): return lax.all_to_all(copies, axis, split_axis=0, concat_axis=0, tiled=True)]
    all_to_all x4 -> x0, blocking collectives: 51.7 us -> none  [the longest x2 37.2 us: sent_to_all(): return lax.all_to_all(copies, axis, split_axis=0, concat_axis=0, tiled=True)]
    all_to_all x8 -> x0, starting transfers between devices: 45.9 us -> none  [the longest x4 19.5 us: sent_to_all(): return lax.all_to_all(copies, axis, split_axis=0, concat_axis=0, tiled=True)]
    dot_general x4 -> x0, matrix products: 15.6 us -> none  [the longest x1 6.53 us: per_device(): lax.dot_general(pair_cols, weighted, (((0,), (0,)), ((), ())), precision=...]
    gather x2 -> x0, local copies, waits for them, and re-layouts: 11.1 us -> none  [the longest x1 5.63 us: per_device(): jnp.take(band_vectors, occ_index, axis=1)]
    mul x3 -> x0, other arithmetic: 5.99 us -> none  [the longest x1 4.43 us: per_device(): jnp.take(band_vectors, occ_index, axis=1)]
    broadcast_in_dim x6 -> x0, local copies, waits for them, and re-layouts: 3.86 us -> none  [sent_to_all(): copies = jnp.broadcast_to(value, (lax.axis_size(axis), *value.shape))]
  transfers between devices with their start and end apart: 8 -> 0, of which waited for: 8 -> 0; matrix products, arithmetic and copies ran while one was open for 6% -> 0% of each run, Pallas kernels for 0% -> 0%
where the time goes in v1:
time: 80.9 us; the launch traced here: 80.7 us
  Pallas kernels  78.1 us (97%)
  local copies, waits for them, and re-layouts  2.59 us (3%)
    pallas_call x1, Pallas kernels, per_device(): pl.pallas_call(main_kernel, out_shape=jax.ShapeDtypeStruct((8, 512), F32)...  66.9 us
    pallas_call x1, Pallas kernels, per_device(): pl.pallas_call(pair_kernel, out_shape=(jax.ShapeDtypeStruct((1536, KB), B...  11.2 us

profile of v1, /device:TPU:1, one launch (start us, length us, event | category | flops | bytes accessed | tf_op | source)
XLA Modules:
  0.0 80.7 jit_solution(10365920351529753571)
XLA Ops:
  0.0 1.3 %reshape.3.c_ref = f32[1,768]{1,0:T(1,128)} reshape(f32[768]{0:T(1024)} %param.8) | data formatting | bytes 6144 | tf_op jit(solution)/shard_map/reshape | solution.py:327
  1.3 11.2 %pairs.1 = (bf16[1536,768]{1,0:T(8,128)(2,1)}, bf16[1536,768]{1,0:T(8,128)(2,1)}, bf16[512,768]{1,0:T(8,128)(2,1)}, bf16[512,768]{1,0:T(8,128)(2,1)}) custom-call(s32[1536]{0:T(1024)} %occ.1, s32[1536]{0:T(1024)} %vir.1, f32[1536]{0:T(1024)} %weight.1, f32[768,1024]{1,0:T(8,128)} %v_ref.1, f32[1,768]{1,0:T(1,128)} %reshape.3.c_ref), custom_call_target="tpu_custom_call" | custom-call | tf_op jit(solution)/shard_map/pairs/pallas_call | solution.py:311
  12.5 66.9 %window.1 = f32[8,512]{1,0:T(8,128)} custom-call(bf16[1536,768]{1,0:T(8,128)(2,1)} %get-tuple-element.9.pt_hi, bf16[1536,768]{1,0:T(8,128)(2,1)} %get-tuple-element.10.pt_lo, bf16[512,768]{1,0:T(8,128)(2,1)} %get-tuple-element.11.w_hi, bf16[512,768]{1,0:T(8,128)(2,1)} %get-tuple-element.12.w_lo, s32[1024]{0:T(1024)} %fidx.1, f32[16]{0:T(128)} %ftab.1), custom_call_target="tpu_custom_call" | custom-call | tf_op jit(solution)/shard_map/window/pallas_call | solution.py:328
  79.4 1.3 %copy.9 = f32[8,512]{1,0:T(8,128)} copy(f32[8,512]{1,0:T(8,128)} %window.1) | data formatting | bytes 32768

commit v2 on v0

v2 whole, which is shorter than its diff:
```python
import math

import jax
import jax.numpy as jnp
from jax import lax
from jax.experimental import pallas as pl
from jax.experimental.pallas import tpu as pltpu
from jax.sharding import Mesh
from jax.sharding import PartitionSpec as P

NB = 49152
ROWS = ("rows_0", "rows_1", "rows_2")
ROWS_COLS = ("rows_0", "rows_1", "rows_2", "cols")
MESH = pl.DeviceIdType.MESH
F32 = jnp.float32
BF16 = jnp.bfloat16
KB = 768
NK = KB // 128
HALF = 768
RELS = [(a, b, d) for a in range(2) for b in range(2) for d in range(2)][1:]
LONG = [(d, h, l) for l in range(2) for d, h in ((0, 0), (1, 1))]
SHORT = [(d, h, l) for l in range(2) for d, h in ((0, 1), (1, 0))]


def split(x):
    hi = x.astype(BF16)
    return hi, (x - hi.astype(F32)).astype(BF16)


def nt(a, b):
    return lax.dot_general(a, b, (((1,), (1,)), ((), ())), preferred_element_type=F32)


def nn(a, b):
    return lax.dot_general(a, b, (((1,), (0,)), ((), ())), preferred_element_type=F32)


def nt3(ah, al, bh, bl):
    return nt(ah, bh) + nt(ah, bl) + nt(al, bh)


def nn3(ah, al, bh, bl):
    return nn(ah, bh) + nn(ah, bl) + nn(al, bh)


def mod(a, n):
    return lax.rem(a + n, n)


def window_kernel(
    occ, vir, fidx, ftab, weight, coulomb, v_hbm, out_ref,
    v_ref, vt, pt, ph, pw, qh, ql, nh, nl,
    r_all, x_all, r_in, x_in,
    zin, yin, rfin, xfin, ry_in, xz_in,
    x32, rfull, yfull, mbuf, m_in, sbuf, s_in,
    load, send, recv,
):
    y = lax.axis_index("rows_0")
    z = lax.axis_index("rows_1")
    c = lax.axis_index("rows_2")
    g = lax.axis_index("grp")
    cl = lax.axis_index("cols")
    plane = 2 * g + cl
    started = []

    def copy(src, dst, to):
        i = len(started)
        d = pltpu.make_async_remote_copy(
            src_ref=src, dst_ref=dst, send_sem=send.at[i], recv_sem=recv.at[i],
            device_id=to, device_id_type=MESH,
        )
        d.start()
        started.append(d)
        return d

    def zto(k):
        return {"rows_1": mod(z + k, 8)}

    def yto(k):
        return {"rows_0": mod(y + k, 4)}

    def xto(rel):
        rg, rc, rl = rel
        return {"grp": mod(g + rg, 2), "rows_2": mod(c + rc, 2), "cols": mod(cl + rl, 2)}

    loads = []
    for k in range(NK):
        rows = pl.ds(k * 128, 128)
        loads.append(pltpu.make_async_copy(v_hbm.at[rows], v_ref.at[rows], load.at[k]))
        loads[k].start()

    barrier = pltpu.get_barrier_semaphore()
    for k in range(1, 8):
        pl.semaphore_signal(barrier, inc=1, device_id=zto(k), device_id_type=MESH)
    for k in range(1, 4):
        pl.semaphore_signal(barrier, inc=1, device_id=yto(k), device_id_type=MESH)
    for rel in RELS:
        pl.semaphore_signal(barrier, inc=1, device_id=xto(rel), device_id_type=MESH)

    for k in range(NK):
        loads[k].wait()
        for nb in range(8):
            block = v_ref[k * 128 : (k + 1) * 128, nb * 128 : (nb + 1) * 128]
            vt[nb * 128 : (nb + 1) * 128, k, :] = block.T

    def gather(base, to):
        def some(i, carry):
            for u in range(16):
                at = i * 16 + u
                pt[to + at] = vt[occ[base + at]] * vt[vir[base + at]]
            return carry

        lax.fori_loop(0, 8, some, 0)

    def weights(base):
        row = weight[pl.ds(pl.multiple_of(base, 128), 128)].reshape(1, 128)
        return jnp.broadcast_to(row, (128, 128)).T

    def cvec(k):
        return coulomb[k * 128 : (k + 1) * 128].reshape(1, 128)

    for s in range(2):
        base = 256 * plane + 128 * s
        gather(base, 128 * s)
        w = weights(base)
        for k in range(NK):
            x = pt[s * 128 : (s + 1) * 128, k, :] * w * cvec(k)
            hi, lo = split(x)
            qh[s * 128 : (s + 1) * 128, k * 128 : (k + 1) * 128] = hi
            ql[s * 128 : (s + 1) * 128, k * 128 : (k + 1) * 128] = lo
    for k in range(NK):
        for m in range(16):
            two = [
                vt[pl.ds(32 * (2 * m + e) + 8 * plane, 8), k, :] for e in range(2)
            ]
            hi, lo = split(jnp.concatenate(two, axis=0) * cvec(k))
            nh[m * 16 : (m + 1) * 16, k * 128 : (k + 1) * 128] = hi
            nl[m * 16 : (m + 1) * 16, k * 128 : (k + 1) * 128] = lo

    def block(t, carry, slot, half):
        for s in range(2):
            base = 512 * t + 256 * s + 128 * half
            gather(base, 128 * s)
            w = weights(base)
            for k in range(NK):
                hi, lo = split(pt[s * 128 : (s + 1) * 128, k, :] * w)
                ph[s * 128 : (s + 1) * 128, k * 128 : (k + 1) * 128] = hi
                pw[s * 128 : (s + 1) * 128, k * 128 : (k + 1) * 128] = lo
        r = nt3(ph[...], pw[...], qh[...], ql[...])
        at = pl.multiple_of(t * 256, 256)
        r_all[slot, 0, pl.ds(at, 256), :] = r[:, 0:128]
        r_all[slot, 1, pl.ds(at, 256), :] = r[:, 128:256]
        x_all[slot, t] = nt3(nh[...], nl[...], ph[...], pw[...])
        return carry

    lax.fori_loop(0, 3, lambda t, a: block(t, a, 0, 1 - c), 0)
    pl.semaphore_wait(barrier, 17)
    core = {"rows_2": 1 - c}
    dr = copy(r_all.at[0], r_in, core)
    dx = copy(x_all.at[0], x_in, core)
    lax.fori_loop(0, 3, lambda t, a: block(t, a, 1, c), 0)

    def zrows(k, start, size):
        return pl.ds(pl.multiple_of(mod(z + k, 8) * 96 + start, 8), size)

    def yrows(k, start, size):
        return pl.ds(pl.multiple_of(mod(y + k, 4) * 64 + start, 8), size)

    sign = (-1, 1)

    def zterm(flow, s):
        d, h, l = flow
        return r_all.at[1, l, zrows(sign[d] * (5 - s), 48 * h, 48)]

    def zhop(flow, s, src):
        d, h, l = flow
        return copy(src, zin.at[d, h, l, s - 1], zto(sign[d]))

    dr.wait_recv()
    r_all[1] += r_in[...]
    zf = {}
    for f in LONG:
        zf[f] = zhop(f, 1, zterm(f, 1))
    for f in SHORT:
        zf[f] = zhop(f, 2, zterm(f, 2))

    def zpass(f, s):
        d, h, l = f
        zf[f].wait_recv()
        zin[d, h, l, s - 1] += zterm(f, s + 1)[...]
        zf[f] = zhop(f, s + 1, zin.at[d, h, l, s - 1])

    def yterm(k, h, q):
        return x_all.at[1, q, yrows(k, 32 * h, 32)]

    dx.wait_recv()
    x_all[1] += x_in[...]
    yl = {}
    ys = {}
    for q in range(3):
        for d in range(2):
            yl[d, q] = copy(yterm(2, d, q), yin.at[d, q, 0], yto(sign[d]))
    for q in range(3):
        for d in range(2):
            ys[d, q] = copy(yterm(sign[d], 1 - d, q), yin.at[d, q, 1], yto(sign[d]))

    for f in LONG:
        zpass(f, 1)
    for q in range(3):
        for d in range(2):
            yl[d, q].wait_recv()
            yin[d, q, 0] += yterm(sign[d], d, q)[...]
            yl[d, q] = copy(yin.at[d, q, 0], yin.at[d, q, 2], yto(sign[d]))
    for f in SHORT:
        zpass(f, 2)
    for f in LONG:
        zpass(f, 2)
    xz = []

    def yfinish(q):
        for d in range(2):
            ys[d, q].wait_recv()
            yl[d, q].wait_recv()
        for h in range(2):
            xfin[q, 32 * h : 32 * h + 32] = (
                yterm(0, h, q)[...] + yin[h, q, 2] + yin[1 - h, q, 1]
            )
        for k in (4, 3, 5, 2, 6, 1, 7):
            rows = pl.ds(pl.multiple_of(mod(z + k, 8) * 8, 8), 8)
            xz.append(copy(xfin.at[q, rows], xz_in.at[k, q], zto(k)))

    for f in SHORT:
        zpass(f, 3)
    yfinish(0)
    for f in LONG:
        zpass(f, 3)
    yfinish(1)
    yfinish(2)
    for f in SHORT:
        zf[f].wait_recv()
    for f in LONG:
        zf[f].wait_recv()
    for h in range(2):
        for l in range(2):
            rfin[l, 48 * h : 48 * h + 48] = (
                r_all[1, l, zrows(0, 48 * h, 48)] + zin[0, h, l, 3] + zin[1, h, l, 3]
            )
    ry = []
    for k in (2, 1, 3):
        rows = pl.ds(pl.multiple_of(mod(y + k, 4) * 24, 8), 24)
        ry.append(copy(rfin.at[:, rows], ry_in.at[k], yto(k)))

    for d in xz:
        d.wait_recv()
    tile = xfin[:, pl.ds(pl.multiple_of(z * 8, 8), 8)]
    for k in range(1, 8):
        tile = tile + xz_in[k]
    chip = y * 8 + z
    row = lax.broadcasted_iota(jnp.int32, (3, 8, 256), 1)
    factor = jnp.zeros((3, 8, 256), F32)
    for i in range(8):
        factor = jnp.where(row == i, ftab[fidx[32 * chip + 8 * plane + i]], factor)
    mine = pl.ds(pl.multiple_of(plane * 8, 8), 8)
    x32[:, mine] = tile * factor * (1.0 / math.sqrt(NB))
    xs = [copy(x32.at[:, mine], x32.at[:, mine], xto(rel)) for rel in ((1, 0, 1), (1, 0, 0), (0, 0, 1))]

    for d in ry:
        d.wait_recv()
    tile = rfin[:, pl.ds(pl.multiple_of(y * 24, 8), 24)]
    for k in range(1, 4):
        tile = tile + ry_in[k]

    def rtile(kz, ky):
        at = (mod(z + kz, 8) * 4 + mod(y + ky, 4)) * 24
        return rfull.at[:, pl.ds(pl.multiple_of(at, 8), 24)]

    rtile(0, 0)[...] = tile * (1.0 / NB)
    ya = {k: copy(rtile(0, 0), rtile(0, 0), yto(k)) for k in (2, 1, 3)}
    za = {}

    def far(d, k):
        return 4 if (k < 2) == (d == 0) else 3

    def zsend(d, k, s):
        src = rtile(-sign[d] * (s - 1), k)
        za[d, k] = copy(src, src, zto(sign[d]))

    for d in range(2):
        zsend(d, 0, 1)

    for d in xs:
        d.wait_recv()
    myrows = pl.multiple_of(chip * 32, 32)
    lanes = pl.ds(pl.multiple_of(lax.rem(plane, 2) * 128, 128), 128)
    yfull[pl.ds(myrows, 32)] = x32[plane // 2, :, lanes]
    ymine = yfull.at[pl.ds(myrows, 32)]
    yz = {k: copy(ymine, ymine, zto(k)) for k in (4, 3, 5, 2, 6, 1, 7)}

    for k in (1, 3, 2):
        ya[k].wait_recv()
        for d in range(2):
            zsend(d, 4 - k, 1)

    yrot = {}

    def ytile(ky, kz):
        at = (mod(y + ky, 4) * 8 + mod(z + kz, 8)) * 32
        return yfull.at[pl.ds(pl.multiple_of(at, 32), 32)]

    def ysend(kz):
        for d in range(2):
            yrot[d, kz] = copy(ytile(0, kz), ytile(0, kz), yto(sign[d]))

    def zforward(s):
        for k in (0, 3, 1, 2):
            for d in range(2):
                if far(d, k) > s:
                    za[d, k].wait_recv()
                    zsend(d, k, s + 1)
                elif far(d, k) == s:
                    za[d, k].wait_recv()

    zforward(1)
    ysend(0)
    for k in (1, 7, 2, 6):
        yz[k].wait_recv()
        ysend(8 - k)
    zforward(2)
    for k in (3, 5, 4):
        yz[k].wait_recv()
        ysend(8 - k)
    last = []
    for kz in (0, 7, 1, 6, 2):
        for d in range(2):
            yrot[d, kz].wait_recv()
            if kz % 2 == d:
                src = ytile(-sign[d], kz)
                last.append(copy(src, src, yto(sign[d])))
    zforward(3)
    for kz in (5, 3, 4):
        for d in range(2):
            yrot[d, kz].wait_recv()
            if kz % 2 == d:
                src = ytile(-sign[d], kz)
                last.append(copy(src, src, yto(sign[d])))
    zforward(4)

    m = jnp.zeros((32, 256), F32)
    for q in range(3):
        xh, xl = split(x32[q])
        rows = slice(256 * q, 256 * q + 256)
        rh, rl = split(jnp.concatenate([rfull[0, rows], rfull[1, rows]], axis=1))
        m = m + nn3(xh, xl, rh, rl)
    mbuf[0] = m[:, 0:128]
    mbuf[1] = m[:, 128:256]
    dm = copy(mbuf.at[1 - c], m_in, core)
    for d in last:
        d.wait_recv()
    yh, yw = split(yfull[...])
    dm.wait_recv()
    mh, ml = split(mbuf[c] + m_in[...])
    s = nt3(mh, ml, yh, yw)
    for tg in range(2):
        for tc in range(2):
            for tl in range(2):
                at = 16 * tc + 8 * tl
                sbuf[tg * 4 + tc * 2 + tl] = s[at : at + 8, tg * 512 : (tg + 1) * 512]
    ds = []
    for i, rel in enumerate(RELS):
        to = xto(rel)
        t = to["grp"] * 4 + to["rows_2"] * 2 + to["cols"]
        ds.append(copy(sbuf.at[t], s_in.at[i], to))
    total = sbuf[g * 4 + c * 2 + cl]
    for i, d in enumerate(ds):
        d.wait_recv()
        total = total + s_in[i]
    out_ref[...] = total * (1.0 / math.sqrt(1024))
    for d in started:
        d.wait_send()


def per_device(band_vectors, coulomb, pair_weight, occ_index, vir_index, freq_index, freq_table):
    smem = pl.BlockSpec(memory_space=pltpu.SMEM)
    vmem = pl.BlockSpec(memory_space=pltpu.VMEM)
    return pl.pallas_call(
        window_kernel,
        out_shape=jax.ShapeDtypeStruct((8, 512), F32),
        in_specs=[smem, smem, smem, smem, vmem, vmem, pl.BlockSpec(memory_space=pl.ANY)],
        out_specs=vmem,
        scratch_shapes=[
            pltpu.VMEM((KB, 1024), F32),
            pltpu.VMEM((1024, 8, 128), F32),
            pltpu.VMEM((256, 8, 128), F32),
            pltpu.VMEM((256, KB), BF16),
            pltpu.VMEM((256, KB), BF16),
            pltpu.VMEM((256, KB), BF16),
            pltpu.VMEM((256, KB), BF16),
            pltpu.VMEM((256, KB), BF16),
            pltpu.VMEM((256, KB), BF16),
            pltpu.VMEM((2, 2, HALF, 128), F32),
            pltpu.VMEM((2, 3, 256, 256), F32),
            pltpu.VMEM((2, HALF, 128), F32),
            pltpu.VMEM((3, 256, 256), F32),
            pltpu.VMEM((2, 2, 2, 4, 48, 128), F32),
            pltpu.VMEM((2, 3, 3, 32, 256), F32),
            pltpu.VMEM((2, 96, 128), F32),
            pltpu.VMEM((3, 64, 256), F32),
            pltpu.VMEM((4, 2, 24, 128), F32),
            pltpu.VMEM((8, 3, 8, 256), F32),
            pltpu.VMEM((3, 32, 256), F32),
            pltpu.VMEM((2, HALF, 128), F32),
            pltpu.VMEM((1024, 128), F32),
            pltpu.VMEM((2, 32, 128), F32),
            pltpu.VMEM((32, 128), F32),
            pltpu.VMEM((8, 8, 512), F32),
            pltpu.VMEM((7, 8, 512), F32),
            pltpu.SemaphoreType.DMA((NK,)),
            pltpu.SemaphoreType.DMA((160,)),
            pltpu.SemaphoreType.DMA((160,)),
        ],
        compiler_params=pltpu.CompilerParams(collective_id=0, has_side_effects=True),
        name="window",
    )(occ_index, vir_index, freq_index, freq_table, pair_weight, coulomb, band_vectors)


def solution(mesh):
    torus = Mesh(
        mesh.devices.reshape(mesh.shape["grp"], 4, 8, 2, mesh.shape["cols"]),
        ("grp", "rows_0", "rows_1", "rows_2", "cols"),
    )
    placed = (P(ROWS, None), P(ROWS), P(), P(), P(), P(), P())
    return jax.shard_map(
        per_device, mesh=torus, in_specs=placed, out_specs=P(ROWS_COLS, "grp"), check_vma=False
    )
```

time: 226 us -> 72.4 us (0.32); the launches traced: 223 us -> 72.2 us
  waiting for transfers between devices: 72.8 us -> 0 us
  Pallas kernels: 0 us -> 70.9 us
  blocking collectives: 51.7 us -> 0 us
  starting transfers between devices: 45.9 us -> 0 us
  local copies, waits for them, and re-layouts: 26.2 us -> 1.32 us
  matrix products: 15.6 us -> 0 us
  other arithmetic: 10.3 us -> 0 us
    all_to_all x8 -> x0, waiting for transfers between devices: 72.8 us -> none  [the longest x4 39.9 us: sent_to_all(): return lax.all_to_all(copies, axis, split_axis=0, concat_axis=0, tiled=True)]
    pallas_call x0 -> x1, Pallas kernels: none -> 70.9 us  [per_device(): pl.pallas_call(window_kernel, out_shape=jax.ShapeDtypeStruct((8, 512), F3...]
    all_to_all x4 -> x0, blocking collectives: 51.7 us -> none  [the longest x2 37.2 us: sent_to_all(): return lax.all_to_all(copies, axis, split_axis=0, concat_axis=0, tiled=True)]
    all_to_all x8 -> x0, starting transfers between devices: 45.9 us -> none  [the longest x4 19.5 us: sent_to_all(): return lax.all_to_all(copies, axis, split_axis=0, concat_axis=0, tiled=True)]
    dot_general x4 -> x0, matrix products: 15.6 us -> none  [the longest x1 6.53 us: per_device(): lax.dot_general(pair_cols, weighted, (((0,), (0,)), ((), ())), precision=...]
    gather x2 -> x0, local copies, waits for them, and re-layouts: 11.1 us -> none  [the longest x1 5.63 us: per_device(): jnp.take(band_vectors, occ_index, axis=1)]
    mul x3 -> x0, other arithmetic: 5.99 us -> none  [the longest x1 4.43 us: per_device(): jnp.take(band_vectors, occ_index, axis=1)]
    broadcast_in_dim x6 -> x0, local copies, waits for them, and re-layouts: 3.86 us -> none  [sent_to_all(): copies = jnp.broadcast_to(value, (lax.axis_size(axis), *value.shape))]
  transfers between devices with their start and end apart: 8 -> 0, of which waited for: 8 -> 0; matrix products, arithmetic and copies ran while one was open for 6% -> 0% of each run, Pallas kernels for 0% -> 0%
where the time goes in v2:
time: 72.4 us; the launch traced here: 72.2 us
  Pallas kernels  70.9 us (98%)
  local copies, waits for them, and re-layouts  1.32 us (2%)
    pallas_call x1, Pallas kernels, per_device(): pl.pallas_call(window_kernel, out_shape=jax.ShapeDtypeStruct((8, 512), F3...  70.9 us

profile of v2, /device:TPU:1, one launch (start us, length us, event | category | flops | bytes accessed | tf_op | source)
XLA Modules:
  0.0 72.2 jit_solution(8661008385214610035)
XLA Ops:
  0.0 70.9 %window.1 = f32[8,512]{1,0:T(8,128)} custom-call(s32[1536]{0:T(1024)} %occ.1, s32[1536]{0:T(1024)} %vir.1, s32[1024]{0:T(1024)} %fidx.1, f32[16]{0:T(128)} %ftab.1, f32[1536]{0:T(1024)} %weight.1, f32[768]{0:T(1024)} %coulomb.1, f32[768,1024]{1,0:T(8,128)} %v_hbm.1), custom_call_target="tpu_custom_call" | custom-call | tf_op jit(solution)/shard_map/window/pallas_call | solution.py:385
  70.9 1.3 %copy.9 = f32[8,512]{1,0:T(8,128)} copy(f32[8,512]{1,0:T(8,128)} %window.1) | data formatting | bytes 32768

commit v3 on v2

v3 whole, which is shorter than its diff:
```python
import math

import jax
import jax.numpy as jnp
from jax import lax
from jax.experimental import pallas as pl
from jax.experimental.pallas import tpu as pltpu
from jax.sharding import Mesh
from jax.sharding import PartitionSpec as P

NB = 49152
ROWS = ("rows_0", "rows_1", "rows_2")
ROWS_COLS = ("rows_0", "rows_1", "rows_2", "cols")
MESH = pl.DeviceIdType.MESH
F32 = jnp.float32
BF16 = jnp.bfloat16
KB = 768
NK = KB // 128
HALF = 768
RELS = [(a, b, d) for a in range(2) for b in range(2) for d in range(2)][1:]
NEAR = [(e, a, b, d) for e in range(4) for a in range(2) for b in range(2) for d in range(2)]


def split(x):
    hi = x.astype(BF16)
    return hi, (x - hi.astype(F32)).astype(BF16)


def nt(a, b):
    return lax.dot_general(a, b, (((1,), (1,)), ((), ())), preferred_element_type=F32)


def nn(a, b):
    return lax.dot_general(a, b, (((1,), (0,)), ((), ())), preferred_element_type=F32)


def nt3(ah, al, bh, bl):
    return nt(ah, bh) + nt(ah, bl) + nt(al, bh)


def nn3(ah, al, bh, bl):
    return nn(ah, bh) + nn(ah, bl) + nn(al, bh)


def mod(a, n):
    return lax.rem(a + n, n)


def window_kernel(
    occ, vir, fidx, ftab, weight, coulomb, v_hbm, out_ref,
    v_ref, vt, pt, ph, pw, qh, ql, nh, nl,
    r_own, r_oth, r_in, x_all, x_in,
    za_in, zb_in, zc_in, zr_in, yin, rfin, xfin, ry_in, xz_in,
    rq, xt, yt, xq, y32, yq, mbuf, m_in, sbuf, s_in,
    load, psend, precv, qsend, qrecv, ssend, srecv, send, recv,
):
    y = lax.axis_index("rows_0")
    z = lax.axis_index("rows_1")
    c = lax.axis_index("rows_2")
    g = lax.axis_index("grp")
    cl = lax.axis_index("cols")
    plane = 2 * g + cl
    started = []

    def copy(src, dst, to):
        i = len(started)
        d = pltpu.make_async_remote_copy(
            src_ref=src, dst_ref=dst, send_sem=send.at[i], recv_sem=recv.at[i],
            device_id=to, device_id_type=MESH,
        )
        d.start()
        started.append(d)
        return d

    def zto(k):
        return {"rows_1": mod(z + k, 8)}

    def yto(k):
        return {"rows_0": mod(y + k, 4)}

    def near(rel):
        ry, rg, rc, rl = rel
        return {
            "rows_0": mod(y + ry, 4), "grp": mod(g + rg, 2),
            "rows_2": mod(c + rc, 2), "cols": mod(cl + rl, 2),
        }

    vt2 = vt.reshape(8192, 128)
    pt2 = pt.reshape(2048, 128)
    loads = []
    for k in range(NK):
        rows = pl.ds(k * 128, 128)
        loads.append(pltpu.make_async_copy(v_hbm.at[rows], v_ref.at[rows], load.at[k]))
        loads[k].start()

    barrier = pltpu.get_barrier_semaphore()
    for k in range(1, 8):
        pl.semaphore_signal(barrier, inc=1, device_id=zto(k), device_id_type=MESH)
    for rel in NEAR[1:]:
        pl.semaphore_signal(barrier, inc=1, device_id=near(rel), device_id_type=MESH)

    for k in range(NK):
        loads[k].wait()
        for nb in range(8):
            block = v_ref[k * 128 : (k + 1) * 128, nb * 128 : (nb + 1) * 128]
            vt2[pl.ds(nb * 1024 + k, 128, stride=8), :] = block.T

    def gather(base, to):
        def some(i, carry):
            for u in range(16):
                at = i * 16 + u
                pt[to + at] = vt[occ[base + at]] * vt[vir[base + at]]
            return carry

        lax.fori_loop(0, 8, some, 0)

    def weights(base):
        row = weight[pl.ds(pl.multiple_of(base, 128), 128)].reshape(1, 128)
        return jnp.broadcast_to(row, (128, 128)).T

    def cvec(k):
        return coulomb[k * 128 : (k + 1) * 128].reshape(1, 128)

    for s in range(2):
        base = 256 * plane + 128 * mod(c + s, 2)
        gather(base, 128 * s)
        w = weights(base)
        for k in range(NK):
            x = pt2[pl.ds(s * 1024 + k, 128, stride=8), :] * w * cvec(k)
            hi, lo = split(x)
            qh[s * 128 : (s + 1) * 128, k * 128 : (k + 1) * 128] = hi
            ql[s * 128 : (s + 1) * 128, k * 128 : (k + 1) * 128] = lo
    for k in range(NK):
        for m in range(16):
            two = [
                vt2[pl.ds((32 * (2 * m + e) + 8 * plane) * 8 + k, 8, stride=8), :] for e in range(2)
            ]
            hi, lo = split(jnp.concatenate(two, axis=0) * cvec(k))
            nh[m * 16 : (m + 1) * 16, k * 128 : (k + 1) * 128] = hi
            nl[m * 16 : (m + 1) * 16, k * 128 : (k + 1) * 128] = lo

    core = {"rows_2": 1 - c}

    def to_partner(i):
        rows = pl.ds(pl.multiple_of(i * 256, 256), 256)
        return pltpu.make_async_remote_copy(
            src_ref=r_oth.at[rows], dst_ref=r_in.at[rows], send_sem=psend.at[i],
            recv_sem=precv.at[i], device_id=core, device_id_type=MESH,
        )

    def block(i, carry):
        half = mod(c + 1 + i // 3, 2)
        t = lax.rem(i, 3)
        for s in range(2):
            base = 512 * t + 256 * s + 128 * half
            gather(base, 128 * s)
            w = weights(base)
            for k in range(NK):
                hi, lo = split(pt2[pl.ds(s * 1024 + k, 128, stride=8), :] * w)
                ph[i, s * 128 : (s + 1) * 128, k * 128 : (k + 1) * 128] = hi
                pw[i, s * 128 : (s + 1) * 128, k * 128 : (k + 1) * 128] = lo
        r = nt3(ph[i], pw[i], qh[...], ql[...])
        n = half * 3 + t
        at = pl.multiple_of(n * 256, 256)
        r_own[pl.ds(at, 256), :] = r[:, 0:128]
        r_oth[pl.ds(at, 256), :] = r[:, 128:256]
        to_partner(n).start()
        return carry

    pl.semaphore_wait(barrier, 38)
    lax.fori_loop(0, 6, block, 0)

    def rpiece(k, ky):
        at = (ky * 8 + mod(z + k, 8)) * 48
        return r_own.at[pl.ds(pl.multiple_of(at, 8), 48)]

    sign = (-1, 1)
    for i in range(6):
        to_partner(i).wait()
    r_own[...] += r_in[...]
    fa = {}
    fb = {}
    fc = {}
    for j in range(2):
        for d in range(2):
            fa[d, j] = copy(rpiece(4 * sign[d], 2 * d + j), za_in.at[d, j], zto(2 * sign[d]))
    for ky in (0, 2, 1, 3):
        for d in range(2):
            fb[d, ky] = copy(rpiece(3 * sign[d], ky), zb_in.at[d, ky], zto(sign[d]))
    for ky in range(4):
        for d in range(2):
            fc[d, ky] = copy(rpiece(sign[d], ky), zc_in.at[d, ky], zto(sign[d]))

    px = []
    for t in range(3):
        x_all[0, t] = nt3(nh[...], nl[...], ph[t], pw[t])
        px.append(copy(x_all.at[0, t], x_in.at[t], core))
    for t in range(3):
        x_all[1, t] = nt3(nh[...], nl[...], ph[3 + t], pw[3 + t])

    def yrows(k, start, size):
        return pl.ds(pl.multiple_of(mod(y + k, 4) * 64 + start, 8), size)

    def yterm(k, h, q):
        return x_all.at[1, q, yrows(k, 32 * h, 32)]

    yl = {}
    ys = {}
    for q in range(3):
        px[q].wait_recv()
        x_all[1, q] += x_in[q]
        for d in range(2):
            yl[d, q] = copy(yterm(2, d, q), yin.at[d, q, 0], yto(sign[d]))
    for q in range(3):
        for d in range(2):
            ys[d, q] = copy(yterm(sign[d], 1 - d, q), yin.at[d, q, 1], yto(sign[d]))

    fr = {}
    for ky in (0, 2, 1, 3):
        for d in range(2):
            fb[d, ky].wait_recv()
            part = zb_in[d, ky] + rpiece(2 * sign[d], ky)[...]
            if ky // 2 == d:
                fa[d, ky % 2].wait_recv()
                part = part + za_in[d, ky % 2]
            zb_in[d, ky] = part
            fr[d, ky] = copy(zb_in.at[d, ky], zr_in.at[d, ky], zto(2 * sign[d]))
    for q in range(3):
        for d in range(2):
            yl[d, q].wait_recv()
            yin[d, q, 0] += yterm(sign[d], d, q)[...]
            yl[d, q] = copy(yin.at[d, q, 0], yin.at[d, q, 2], yto(sign[d]))

    for ky in (0, 2, 1, 3):
        part = rpiece(0, ky)[...]
        for d in range(2):
            fc[d, ky].wait_recv()
            fr[d, ky].wait_recv()
            part = part + (zc_in[d, ky] + zr_in[d, ky])
        rfin[ky] = part
    ry = [copy(rfin.at[mod(y + k, 4)], ry_in.at[k], yto(k)) for k in (2, 1, 3)]

    xz = []
    for q in range(3):
        for d in range(2):
            ys[d, q].wait_recv()
            yl[d, q].wait_recv()
        for h in range(2):
            xfin[q, 32 * h : 32 * h + 32] = (
                yterm(0, h, q)[...] + yin[h, q, 2] + yin[1 - h, q, 1]
            )
        for k in (4, 3, 5, 2, 6, 1, 7):
            rows = pl.ds(pl.multiple_of(mod(z + k, 8) * 8, 8), 8)
            xz.append(copy(xfin.at[q, rows], xz_in.at[k, q], zto(k)))

    for d in ry:
        d.wait_recv()
    rq[z] = (rfin[y] + (ry_in[1] + ry_in[2] + ry_in[3])) * (1.0 / NB)
    rz = [copy(rq.at[z], rq.at[z], zto(k)) for k in (4, 3, 5, 2, 6, 1, 7)]

    for d in xz:
        d.wait_recv()
    tile = xfin[:, pl.ds(pl.multiple_of(z * 8, 8), 8)]
    for k in range(1, 8):
        tile = tile + xz_in[k]
    chip = y * 8 + z
    row = lax.broadcasted_iota(jnp.int32, (3, 8, 256), 1)
    factor = jnp.zeros((3, 8, 256), F32)
    for i in range(8):
        factor = jnp.where(row == i, ftab[fidx[32 * chip + 8 * plane + i]], factor)
    tile = tile * factor * (1.0 / math.sqrt(NB))
    xt[0] = jnp.concatenate([tile[0], tile[1][:, 0:128]], axis=1)
    xt[1] = jnp.concatenate([tile[1][:, 128:256], tile[2]], axis=1)
    for j in range(4):
        yt[j] = tile[j // 2][:, 128 * (j % 2) : 128 * (j % 2) + 128]

    def quarter(i, rel, e):
        rg, rc, rl = rel
        to = {"grp": mod(g + rg, 2), "rows_2": mod(c + rc, 2), "cols": mod(cl + rl, 2)}
        to["rows_0"] = 2 * c + e
        return pltpu.make_async_remote_copy(
            src_ref=xt.at[e], dst_ref=xq.at[y, plane], send_sem=qsend.at[i],
            recv_sem=qrecv.at[y, plane], device_id=to, device_id_type=MESH,
        )

    quarters = [(rel, e) for e in range(2) for rel in [(0, 0, 0)] + RELS]
    for i, (rel, e) in enumerate(quarters):
        if rel == (0, 0, 0):

            @pl.when(y != 2 * c + e)
            def _(i=i, rel=rel, e=e):
                quarter(i, rel, e).start()

            @pl.when(y == 2 * c + e)
            def _(e=e):
                xq[y, plane] = xt[e]
        else:
            quarter(i, rel, e).start()
    yx = []
    for rg, rl in ((1, 1), (1, 0), (0, 1)):
        to = {"grp": mod(g + rg, 2), "cols": mod(cl + rl, 2)}
        yx.append(copy(yt.at[2 * to["grp"] + to["cols"]], y32.at[plane], to))
    y32[plane] = yt[plane]
    for d in yx:
        d.wait_recv()
    for j in range(4):
        yq[z, 8 * j : 8 * j + 8] = y32[j]
    yz = [copy(yq.at[z], yq.at[z], zto(k)) for k in (4, 3, 5, 2, 6, 1, 7)]

    for d in rz:
        d.wait_recv()
    for ys_ in range(4):
        for j in range(4):

            def arrived(ys_=ys_, j=j):
                pltpu.make_async_remote_copy(
                    src_ref=xt.at[0], dst_ref=xq.at[ys_, j], send_sem=qsend.at[0],
                    recv_sem=qrecv.at[ys_, j], device_id=core, device_id_type=MESH,
                ).wait_recv()

            own = (ys_ == y) & (j == plane) & (c == y // 2)
            pl.when(jnp.logical_not(own))(arrived)

    xh, xl = split(xq[...].reshape(128, 384))
    rh, rl_ = split(rq[...].reshape(384, 128))
    mbuf[...] = nn3(xh, xl, rh, rl_)
    my = [copy(mbuf, m_in.at[k], yto(k)) for k in (2, 1, 3)]
    for d in yz:
        d.wait_recv()
    yh, yw = split(yq[...].reshape(256, 128))
    for d in my:
        d.wait_recv()
    mh, ml = split(mbuf[...] + (m_in[1] + m_in[2] + m_in[3]))
    s = nt3(mh, ml, yh, yw)
    for i in range(16):
        sbuf[i] = s[8 * i : 8 * i + 8, :]

    e = lax.rem(y, 2)

    def result(i, ry_, rc, rl):
        to = {
            "grp": y // 2, "rows_0": mod(y + ry_, 4), "rows_2": mod(c + rc, 2), "cols": mod(cl + rl, 2),
        }
        src = to["rows_0"] * 4 + to["rows_2"] * 2 + to["cols"]
        return pltpu.make_async_remote_copy(
            src_ref=sbuf.at[src], dst_ref=s_in.at[e, plane, c], send_sem=ssend.at[i],
            recv_sem=srecv.at[e, plane, c], device_id=to, device_id_type=MESH,
        )

    results = [(a, b, d) for a in (0, 2, 1, 3) for b in range(2) for d in range(2)]
    for i, rel in enumerate(results):
        if rel == (0, 0, 0):

            @pl.when(y // 2 != g)
            def _(i=i, rel=rel):
                result(i, *rel).start()

            @pl.when(y // 2 == g)
            def _():
                s_in[e, plane, c] = sbuf[y * 4 + c * 2 + cl]
        else:
            result(i, *rel).start()
    for e_ in range(2):
        for j in range(4):
            for cs in range(2):

                def landed(e_=e_, j=j, cs=cs):
                    pltpu.make_async_remote_copy(
                        src_ref=sbuf.at[0], dst_ref=s_in.at[e_, j, cs], send_sem=ssend.at[0],
                        recv_sem=srecv.at[e_, j, cs], device_id=core, device_id_type=MESH,
                    ).wait_recv()

                own = (e_ == e) & (j == plane) & (cs == c) & (y // 2 == g)
                pl.when(jnp.logical_not(own))(landed)
    for e_ in range(2):
        total = s_in[e_, 0, 0]
        for n in range(1, 8):
            total = total + s_in[e_, n // 2, n % 2]
        out_ref[:, 256 * e_ : 256 * e_ + 256] = total * (1.0 / math.sqrt(1024))

    for i, (rel, e_) in enumerate(quarters):
        if rel == (0, 0, 0):

            @pl.when(y != 2 * c + e_)
            def _(i=i, rel=rel, e_=e_):
                quarter(i, rel, e_).wait_send()
        else:
            quarter(i, rel, e_).wait_send()
    for i, rel in enumerate(results):
        if rel == (0, 0, 0):

            @pl.when(y // 2 != g)
            def _(i=i, rel=rel):
                result(i, *rel).wait_send()
        else:
            result(i, *rel).wait_send()
    for d in started:
        d.wait_send()


def per_device(band_vectors, coulomb, pair_weight, occ_index, vir_index, freq_index, freq_table):
    smem = pl.BlockSpec(memory_space=pltpu.SMEM)
    vmem = pl.BlockSpec(memory_space=pltpu.VMEM)
    return pl.pallas_call(
        window_kernel,
        out_shape=jax.ShapeDtypeStruct((8, 512), F32),
        in_specs=[smem, smem, smem, smem, vmem, vmem, pl.BlockSpec(memory_space=pl.ANY)],
        out_specs=vmem,
        scratch_shapes=[
            pltpu.VMEM((KB, 1024), F32),
            pltpu.VMEM((1024, 8, 128), F32),
            pltpu.VMEM((256, 8, 128), F32),
            pltpu.VMEM((6, 256, KB), BF16),
            pltpu.VMEM((6, 256, KB), BF16),
            pltpu.VMEM((256, KB), BF16),
            pltpu.VMEM((256, KB), BF16),
            pltpu.VMEM((256, KB), BF16),
            pltpu.VMEM((256, KB), BF16),
            pltpu.VMEM((1536, 128), F32),
            pltpu.VMEM((1536, 128), F32),
            pltpu.VMEM((1536, 128), F32),
            pltpu.VMEM((2, 3, 256, 256), F32),
            pltpu.VMEM((3, 256, 256), F32),
            pltpu.VMEM((2, 2, 48, 128), F32),
            pltpu.VMEM((2, 4, 48, 128), F32),
            pltpu.VMEM((2, 4, 48, 128), F32),
            pltpu.VMEM((2, 4, 48, 128), F32),
            pltpu.VMEM((2, 3, 3, 32, 256), F32),
            pltpu.VMEM((4, 48, 128), F32),
            pltpu.VMEM((3, 64, 256), F32),
            pltpu.VMEM((4, 48, 128), F32),
            pltpu.VMEM((8, 3, 8, 256), F32),
            pltpu.VMEM((8, 48, 128), F32),
            pltpu.VMEM((2, 8, 384), F32),
            pltpu.VMEM((4, 8, 128), F32),
            pltpu.VMEM((4, 4, 8, 384), F32),
            pltpu.VMEM((4, 8, 128), F32),
            pltpu.VMEM((8, 32, 128), F32),
            pltpu.VMEM((128, 128), F32),
            pltpu.VMEM((4, 128, 128), F32),
            pltpu.VMEM((16, 8, 256), F32),
            pltpu.VMEM((2, 4, 2, 8, 256), F32),
            pltpu.SemaphoreType.DMA((NK,)),
            pltpu.SemaphoreType.DMA((6,)),
            pltpu.SemaphoreType.DMA((6,)),
            pltpu.SemaphoreType.DMA((16,)),
            pltpu.SemaphoreType.DMA((4, 4)),
            pltpu.SemaphoreType.DMA((16,)),
            pltpu.SemaphoreType.DMA((2, 4, 2)),
            pltpu.SemaphoreType.DMA((112,)),
            pltpu.SemaphoreType.DMA((112,)),
        ],
        compiler_params=pltpu.CompilerParams(collective_id=0, has_side_effects=True),
        name="window",
    )(occ_index, vir_index, freq_index, freq_table, pair_weight, coulomb, band_vectors)


def solution(mesh):
    torus = Mesh(
        mesh.devices.reshape(mesh.shape["grp"], 4, 8, 2, mesh.shape["cols"]),
        ("grp", "rows_0", "rows_1", "rows_2", "cols"),
    )
    placed = (P(ROWS, None), P(ROWS), P(), P(), P(), P(), P())
    return jax.shard_map(
        per_device, mesh=torus, in_specs=placed, out_specs=P(ROWS_COLS, "grp"), check_vma=False
    )
```

time: 72.4 us -> 64.1 us (0.89)
  Pallas kernels: 70.9 us -> 62.2 us
    pallas_call x1, Pallas kernels: 70.9 us -> 62.2 us  [per_device(): pl.pallas_call(window_kernel, out_shape=jax.ShapeDtypeStruct((8, 512), F3...]
where the time goes in v3:
time: 64.1 us; the launch traced here: 63.6 us
  Pallas kernels  62.2 us (97%)
  local copies, waits for them, and re-layouts  1.32 us (2%)
    pallas_call x1, Pallas kernels, per_device(): pl.pallas_call(window_kernel, out_shape=jax.ShapeDtypeStruct((8, 512), F3...  62.2 us
    unnamed x1, local copies, waits for them, and re-layouts  1.32 us

profile of v3, /device:TPU:1, one launch (start us, length us, event | category | flops | bytes accessed | tf_op | source)
XLA Modules:
  0.0 63.6 jit_solution(2876164983937505982)
XLA Ops:
  0.0 62.2 %window.1 = f32[8,512]{1,0:T(8,128)} custom-call(s32[1536]{0:T(1024)} %occ.1, s32[1536]{0:T(1024)} %vir.1, s32[1024]{0:T(1024)} %fidx.1, f32[16]{0:T(128)} %ftab.1, f32[1536]{0:T(1024)} %weight.1, f32[768]{0:T(1024)} %coulomb.1, f32[768,1024]{1,0:T(8,128)} %v_hbm.1), custom_call_target="tpu_custom_call" | custom-call | tf_op jit(solution)/shard_map/window/pallas_call | solution.py:404
  62.2 1.3 %copy.9 = f32[8,512]{1,0:T(8,128)} copy(f32[8,512]{1,0:T(8,128)} %window.1) | data formatting | bytes 32768

commit v4 on v3

--- a/solution.py
+++ b/solution.py
@@ -105,14 +105,16 @@
             block = v_ref[k * 128 : (k + 1) * 128, nb * 128 : (nb + 1) * 128]
             vt2[pl.ds(nb * 1024 + k, 128, stride=8), :] = block.T
 
+    def gather_some(base, to, count):
+        for u in range(count):
+            pt[to + u] = vt[occ[base + u]] * vt[vir[base + u]]
+
     def gather(base, to):
         def some(i, carry):
-            for u in range(16):
-                at = i * 16 + u
-                pt[to + at] = vt[occ[base + at]] * vt[vir[base + at]]
+            gather_some(base + i * 32, to + i * 32, 32)
             return carry
 
-        lax.fori_loop(0, 8, some, 0)
+        lax.fori_loop(0, 4, some, 0)
 
     def weights(base):
         row = weight[pl.ds(pl.multiple_of(base, 128), 128)].reshape(1, 128)
@@ -130,6 +132,54 @@
             hi, lo = split(x)
             qh[s * 128 : (s + 1) * 128, k * 128 : (k + 1) * 128] = hi
             ql[s * 128 : (s + 1) * 128, k * 128 : (k + 1) * 128] = lo
+    core = {"rows_2": 1 - c}
+
+    def to_partner(i):
+        rows = pl.ds(pl.multiple_of(i * 256, 256), 256)
+        return pltpu.make_async_remote_copy(
+            src_ref=r_oth.at[rows], dst_ref=r_in.at[rows], send_sem=psend.at[i],
+            recv_sem=precv.at[i], device_id=core, device_id_type=MESH,
+        )
+
+    def place(i):
+        half = mod(c + 1 + i // 3, 2)
+        t = lax.rem(i, 3)
+        return half * 3 + t, [512 * t + 256 * s + 128 * half for s in range(2)]
+
+    def rows_of(i, bases):
+        for s in range(2):
+            w = weights(bases[s])
+            for k in range(NK):
+                hi, lo = split(pt2[pl.ds(s * 1024 + k, 128, stride=8), :] * w)
+                ph[i, s * 128 : (s + 1) * 128, k * 128 : (k + 1) * 128] = hi
+                pw[i, s * 128 : (s + 1) * 128, k * 128 : (k + 1) * 128] = lo
+
+    def response_of(i, n):
+        r = nt3(ph[i], pw[i], qh[...], ql[...])
+        at = pl.multiple_of(n * 256, 256)
+        r_own[pl.ds(at, 256), :] = r[:, 0:128]
+        r_oth[pl.ds(at, 256), :] = r[:, 128:256]
+
+    def block(i, carry):
+        n, _ = place(i - 1)
+        _, bases = place(i)
+        for s in range(2):
+            gather_some(bases[s], 128 * s, 128)
+        response_of(i - 1, n)
+        to_partner(n).start()
+        rows_of(i, bases)
+        return carry
+
+    first, bases = place(0)
+    for s in range(2):
+        gather(bases[s], 128 * s)
+    rows_of(0, bases)
+    pl.semaphore_wait(barrier, 38)
+    lax.fori_loop(1, 6, block, 0)
+    n, _ = place(5)
+    response_of(5, n)
+    to_partner(n).start()
+
     for k in range(NK):
         for m in range(16):
             two = [
@@ -138,37 +188,6 @@
             hi, lo = split(jnp.concatenate(two, axis=0) * cvec(k))
             nh[m * 16 : (m + 1) * 16, k * 128 : (k + 1) * 128] = hi
             nl[m * 16 : (m + 1) * 16, k * 128 : (k + 1) * 128] = lo
-
-    core = {"rows_2": 1 - c}
-
-    def to_partner(i):
-        rows = pl.ds(pl.multiple_of(i * 256, 256), 256)
-        return pltpu.make_async_remote_copy(
-            src_ref=r_oth.at[rows], dst_ref=r_in.at[rows], send_sem=psend.at[i],
-            recv_sem=precv.at[i], device_id=core, device_id_type=MESH,
-        )
-
-    def block(i, carry):
-        half = mod(c + 1 + i // 3, 2)
-        t = lax.rem(i, 3)
-        for s in range(2):
-            base = 512 * t + 256 * s + 128 * half
-            gather(base, 128 * s)
-            w = weights(base)
-            for k in range(NK):
-                hi, lo = split(pt2[pl.ds(s * 1024 + k, 128, stride=8), :] * w)
-                ph[i, s * 128 : (s + 1) * 128, k * 128 : (k + 1) * 128] = hi
-                pw[i, s * 128 : (s + 1) * 128, k * 128 : (k + 1) * 128] = lo
-        r = nt3(ph[i], pw[i], qh[...], ql[...])
-        n = half * 3 + t
-        at = pl.multiple_of(n * 256, 256)
-        r_own[pl.ds(at, 256), :] = r[:, 0:128]
-        r_oth[pl.ds(at, 256), :] = r[:, 128:256]
-        to_partner(n).start()
-        return carry
-
-    pl.semaphore_wait(barrier, 38)
-    lax.fori_loop(0, 6, block, 0)
 
     def rpiece(k, ky):
         at = (ky * 8 + mod(z + k, 8)) * 48

time: 64.1 us -> 62.4 us (0.973)
  Pallas kernels: 62.2 us -> 60.9 us
    pallas_call x1, Pallas kernels: 62.2 us -> 60.9 us  [per_device(): pl.pallas_call(window_kernel, out_shape=jax.ShapeDtypeStruct((8, 512), F3...]
where the time goes in v4:
time: 62.4 us; the launch traced here: 62.3 us
  Pallas kernels  60.9 us (98%)
  local copies, waits for them, and re-layouts  1.32 us (2%)
    pallas_call x1, Pallas kernels, per_device(): pl.pallas_call(window_kernel, out_shape=jax.ShapeDtypeStruct((8, 512), F3...  60.9 us
    unnamed x1, local copies, waits for them, and re-layouts  1.32 us

profile of v4, /device:TPU:1, one launch (start us, length us, event | category | flops | bytes accessed | tf_op | source)
XLA Modules:
  0.0 62.3 jit_solution(7250217834035980781)
XLA Ops:
  0.0 60.9 %window.1 = f32[8,512]{1,0:T(8,128)} custom-call(s32[1536]{0:T(1024)} %occ.1, s32[1536]{0:T(1024)} %vir.1, s32[1024]{0:T(1024)} %fidx.1, f32[16]{0:T(128)} %ftab.1, f32[1536]{0:T(1024)} %weight.1, f32[768]{0:T(1024)} %coulomb.1, f32[768,1024]{1,0:T(8,128)} %v_hbm.1), custom_call_target="tpu_custom_call" | custom-call | tf_op jit(solution)/shard_map/window/pallas_call | solution.py:423
  60.9 1.3 %copy.9 = f32[8,512]{1,0:T(8,128)} copy(f32[8,512]{1,0:T(8,128)} %window.1) | data formatting | bytes 32768

commit v5 on v4

--- a/solution.py
+++ b/solution.py
@@ -48,7 +48,7 @@
 
 def window_kernel(
     occ, vir, fidx, ftab, weight, coulomb, v_hbm, out_ref,
-    v_ref, vt, pt, ph, pw, qh, ql, nh, nl,
+    v_ref, vt, pt, qt, ph, pw, qh, ql, nh, nl,
     r_own, r_oth, r_in, x_all, x_in,
     za_in, zb_in, zc_in, zr_in, yin, rfin, xfin, ry_in, xz_in,
     rq, xt, yt, xq, y32, yq, mbuf, m_in, sbuf, s_in,
@@ -86,7 +86,8 @@
         }
 
     vt2 = vt.reshape(8192, 128)
-    pt2 = pt.reshape(2048, 128)
+    pts = (pt, qt)
+    pt2s = (pt.reshape(2048, 128), qt.reshape(2048, 128))
     loads = []
     for k in range(NK):
         rows = pl.ds(k * 128, 128)
@@ -105,9 +106,9 @@
             block = v_ref[k * 128 : (k + 1) * 128, nb * 128 : (nb + 1) * 128]
             vt2[pl.ds(nb * 1024 + k, 128, stride=8), :] = block.T
 
-    def gather_some(base, to, count):
+    def gather_some(base, to, count, rows=pt):
         for u in range(count):
-            pt[to + u] = vt[occ[base + u]] * vt[vir[base + u]]
+            rows[to + u] = vt[occ[base + u]] * vt[vir[base + u]]
 
     def gather(base, to):
         def some(i, carry):
@@ -128,7 +129,7 @@
         gather(base, 128 * s)
         w = weights(base)
         for k in range(NK):
-            x = pt2[pl.ds(s * 1024 + k, 128, stride=8), :] * w * cvec(k)
+            x = pt2s[0][pl.ds(s * 1024 + k, 128, stride=8), :] * w * cvec(k)
             hi, lo = split(x)
             qh[s * 128 : (s + 1) * 128, k * 128 : (k + 1) * 128] = hi
             ql[s * 128 : (s + 1) * 128, k * 128 : (k + 1) * 128] = lo
@@ -143,14 +144,14 @@
 
     def place(i):
         half = mod(c + 1 + i // 3, 2)
-        t = lax.rem(i, 3)
+        t = i % 3
         return half * 3 + t, [512 * t + 256 * s + 128 * half for s in range(2)]
 
     def rows_of(i, bases):
         for s in range(2):
             w = weights(bases[s])
             for k in range(NK):
-                hi, lo = split(pt2[pl.ds(s * 1024 + k, 128, stride=8), :] * w)
+                hi, lo = split(pt2s[i % 2][pl.ds(s * 1024 + k, 128, stride=8), :] * w)
                 ph[i, s * 128 : (s + 1) * 128, k * 128 : (k + 1) * 128] = hi
                 pw[i, s * 128 : (s + 1) * 128, k * 128 : (k + 1) * 128] = lo
 
@@ -160,25 +161,18 @@
         r_own[pl.ds(at, 256), :] = r[:, 0:128]
         r_oth[pl.ds(at, 256), :] = r[:, 128:256]
 
-    def block(i, carry):
-        n, _ = place(i - 1)
-        _, bases = place(i)
-        for s in range(2):
-            gather_some(bases[s], 128 * s, 128)
-        response_of(i - 1, n)
-        to_partner(n).start()
-        rows_of(i, bases)
-        return carry
-
-    first, bases = place(0)
-    for s in range(2):
-        gather(bases[s], 128 * s)
-    rows_of(0, bases)
-    pl.semaphore_wait(barrier, 38)
-    lax.fori_loop(1, 6, block, 0)
-    n, _ = place(5)
-    response_of(5, n)
-    to_partner(n).start()
+    for i in range(8):
+        if i == 2:
+            pl.semaphore_wait(barrier, 38)
+        if i < 6:
+            for e in range(2):
+                gather_some(place(i)[1][e], 128 * e, 128, pts[i % 2])
+        if 1 <= i < 7:
+            rows_of(i - 1, place(i - 1)[1])
+        if i >= 2:
+            n, _ = place(i - 2)
+            response_of(i - 2, n)
+            to_partner(n).start()
 
     for k in range(NK):
         for m in range(16):
@@ -428,6 +422,7 @@
         scratch_shapes=[
             pltpu.VMEM((KB, 1024), F32),
             pltpu.VMEM((1024, 8, 128), F32),
+            pltpu.VMEM((256, 8, 128), F32),
             pltpu.VMEM((256, 8, 128), F32),
             pltpu.VMEM((6, 256, KB), BF16),
             pltpu.VMEM((6, 256, KB), BF16),

time: 62.4 us -> 61.6 us (0.987)
  Pallas kernels: 60.9 us -> 60.1 us
    pallas_call x1, Pallas kernels: 60.9 us -> 60.1 us  [per_device(): pl.pallas_call(window_kernel, out_shape=jax.ShapeDtypeStruct((8, 512), F3...]
where the time goes in v5:
time: 61.6 us; the launch traced here: 61.4 us
  Pallas kernels  60.1 us (98%)
  local copies, waits for them, and re-layouts  1.32 us (2%)
    pallas_call x1, Pallas kernels, per_device(): pl.pallas_call(window_kernel, out_shape=jax.ShapeDtypeStruct((8, 512), F3...  60.1 us
    unnamed x1, local copies, waits for them, and re-layouts  1.32 us

profile of v5, /device:TPU:1, one launch (start us, length us, event | category | flops | bytes accessed | tf_op | source)
XLA Modules:
  0.0 61.4 jit_solution(220522700978290300)
XLA Ops:
  0.0 60.1 %window.1 = f32[8,512]{1,0:T(8,128)} custom-call(s32[1536]{0:T(1024)} %occ.1, s32[1536]{0:T(1024)} %vir.1, s32[1024]{0:T(1024)} %fidx.1, f32[16]{0:T(128)} %ftab.1, f32[1536]{0:T(1024)} %weight.1, f32[768]{0:T(1024)} %coulomb.1, f32[768,1024]{1,0:T(8,128)} %v_hbm.1), custom_call_target="tpu_custom_call" | custom-call | tf_op jit(solution)/shard_map/window/pallas_call | solution.py:417
  60.1 1.3 %copy.9 = f32[8,512]{1,0:T(8,128)} copy(f32[8,512]{1,0:T(8,128)} %window.1) | data formatting | bytes 32768

commit v6 on v5

--- a/solution.py
+++ b/solution.py
@@ -51,8 +51,8 @@
     v_ref, vt, pt, qt, ph, pw, qh, ql, nh, nl,
     r_own, r_oth, r_in, x_all, x_in,
     za_in, zb_in, zc_in, zr_in, yin, rfin, xfin, ry_in, xz_in,
-    rq, xt, yt, xq, y32, yq, mbuf, m_in, sbuf, s_in,
-    load, psend, precv, qsend, qrecv, ssend, srecv, send, recv,
+    rq, xt, yt, xq, y32, yq, mbuf, m_in, sbuf, s_pair, s_in,
+    load, psend, precv, xpsend, xprecv, qsend, qrecv, ssend, srecv, send, recv,
 ):
     y = lax.axis_index("rows_0")
     z = lax.axis_index("rows_1")
@@ -124,15 +124,29 @@
     def cvec(k):
         return coulomb[k * 128 : (k + 1) * 128].reshape(1, 128)
 
+    window = [256 * plane + 128 * mod(c + s, 2) for s in range(2)]
     for s in range(2):
-        base = 256 * plane + 128 * mod(c + s, 2)
-        gather(base, 128 * s)
-        w = weights(base)
+        gather(window[s], 128 * s)
+
+    def window_rows():
+        for s in range(2):
+            w = weights(window[s])
+            for k in range(NK):
+                x = pt2s[0][pl.ds(s * 1024 + k, 128, stride=8), :] * w * cvec(k)
+                hi, lo = split(x)
+                qh[s * 128 : (s + 1) * 128, k * 128 : (k + 1) * 128] = hi
+                ql[s * 128 : (s + 1) * 128, k * 128 : (k + 1) * 128] = lo
+
+    def band_rows():
         for k in range(NK):
-            x = pt2s[0][pl.ds(s * 1024 + k, 128, stride=8), :] * w * cvec(k)
-            hi, lo = split(x)
-            qh[s * 128 : (s + 1) * 128, k * 128 : (k + 1) * 128] = hi
-            ql[s * 128 : (s + 1) * 128, k * 128 : (k + 1) * 128] = lo
+            for m in range(16):
+                two = [
+                    vt2[pl.ds((32 * (2 * m + e) + 8 * plane) * 8 + k, 8, stride=8), :] for e in range(2)
+                ]
+                hi, lo = split(jnp.concatenate(two, axis=0) * cvec(k))
+                nh[m * 16 : (m + 1) * 16, k * 128 : (k + 1) * 128] = hi
+                nl[m * 16 : (m + 1) * 16, k * 128 : (k + 1) * 128] = lo
+
     core = {"rows_2": 1 - c}
 
     def to_partner(i):
@@ -143,85 +157,87 @@
         )
 
     def place(i):
-        half = mod(c + 1 + i // 3, 2)
-        t = i % 3
-        return half * 3 + t, [512 * t + 256 * s + 128 * half for s in range(2)]
+        return [512 * (i % 3) + 256 * s + 128 * (i // 3) for s in range(2)]
 
     def rows_of(i, bases):
         for s in range(2):
             w = weights(bases[s])
             for k in range(NK):
-                hi, lo = split(pt2s[i % 2][pl.ds(s * 1024 + k, 128, stride=8), :] * w)
+                hi, lo = split(pt2s[(i + 1) % 2][pl.ds(s * 1024 + k, 128, stride=8), :] * w)
                 ph[i, s * 128 : (s + 1) * 128, k * 128 : (k + 1) * 128] = hi
                 pw[i, s * 128 : (s + 1) * 128, k * 128 : (k + 1) * 128] = lo
 
-    def response_of(i, n):
+    def response_of(i):
         r = nt3(ph[i], pw[i], qh[...], ql[...])
-        at = pl.multiple_of(n * 256, 256)
-        r_own[pl.ds(at, 256), :] = r[:, 0:128]
-        r_oth[pl.ds(at, 256), :] = r[:, 128:256]
+        r_own[i * 256 : (i + 1) * 256, :] = r[:, 0:128]
+        r_oth[i * 256 : (i + 1) * 256, :] = r[:, 128:256]
+
+    def rpiece(k, ky):
+        at = (ky * 8 + mod(z + k, 8)) * 48
+        return r_own.at[pl.ds(pl.multiple_of(at, 8), 48)]
+
+    sign = (-1, 1)
+    fa = {}
+    fb = {}
+    fc = {}
+
+    def start_sums(half):
+        for i in range(3):
+            to_partner(3 * half + i).wait()
+        rows = slice(768 * half, 768 * half + 768)
+        r_own[rows] += r_in[rows]
+        for j in range(2):
+            ky = 2 * half + j
+            fa[half, j] = copy(rpiece(4 * sign[half], ky), za_in.at[half, j], zto(2 * sign[half]))
+        for ky in (2 * half, 2 * half + 1):
+            for d in range(2):
+                fb[d, ky] = copy(rpiece(3 * sign[d], ky), zb_in.at[d, ky], zto(sign[d]))
+        for ky in (2 * half, 2 * half + 1):
+            for d in range(2):
+                fc[d, ky] = copy(rpiece(sign[d], ky), zc_in.at[d, ky], zto(sign[d]))
+
+    def coupling_pair(i):
+        return pltpu.make_async_remote_copy(
+            src_ref=x_all.at[i], dst_ref=x_in.at[i % 3], send_sem=xpsend.at[i % 3],
+            recv_sem=xprecv.at[i % 3], device_id=core, device_id_type=MESH,
+        )
 
     for i in range(8):
         if i == 2:
             pl.semaphore_wait(barrier, 38)
         if i < 6:
             for e in range(2):
-                gather_some(place(i)[1][e], 128 * e, 128, pts[i % 2])
+                gather_some(place(i)[e], 128 * e, 128, pts[(i + 1) % 2])
+        if i == 0:
+            window_rows()
+        if i == 1:
+            band_rows()
         if 1 <= i < 7:
-            rows_of(i - 1, place(i - 1)[1])
+            rows_of(i - 1, place(i - 1))
         if i >= 2:
-            n, _ = place(i - 2)
-            response_of(i - 2, n)
+            n = i - 2
+            response_of(n)
+            x_all[n] = nt3(nh[...], nl[...], ph[n], pw[n])
             to_partner(n).start()
 
-    for k in range(NK):
-        for m in range(16):
-            two = [
-                vt2[pl.ds((32 * (2 * m + e) + 8 * plane) * 8 + k, 8, stride=8), :] for e in range(2)
-            ]
-            hi, lo = split(jnp.concatenate(two, axis=0) * cvec(k))
-            nh[m * 16 : (m + 1) * 16, k * 128 : (k + 1) * 128] = hi
-            nl[m * 16 : (m + 1) * 16, k * 128 : (k + 1) * 128] = lo
-
-    def rpiece(k, ky):
-        at = (ky * 8 + mod(z + k, 8)) * 48
-        return r_own.at[pl.ds(pl.multiple_of(at, 8), 48)]
-
-    sign = (-1, 1)
-    for i in range(6):
-        to_partner(i).wait()
-    r_own[...] += r_in[...]
-    fa = {}
-    fb = {}
-    fc = {}
-    for j in range(2):
-        for d in range(2):
-            fa[d, j] = copy(rpiece(4 * sign[d], 2 * d + j), za_in.at[d, j], zto(2 * sign[d]))
-    for ky in (0, 2, 1, 3):
-        for d in range(2):
-            fb[d, ky] = copy(rpiece(3 * sign[d], ky), zb_in.at[d, ky], zto(sign[d]))
-    for ky in range(4):
-        for d in range(2):
-            fc[d, ky] = copy(rpiece(sign[d], ky), zc_in.at[d, ky], zto(sign[d]))
-
-    px = []
-    for t in range(3):
-        x_all[0, t] = nt3(nh[...], nl[...], ph[t], pw[t])
-        px.append(copy(x_all.at[0, t], x_in.at[t], core))
-    for t in range(3):
-        x_all[1, t] = nt3(nh[...], nl[...], ph[3 + t], pw[3 + t])
+            @pl.when(c != n // 3)
+            def _(n=n):
+                coupling_pair(n).start()
+        if i == 5:
+            start_sums(0)
+    start_sums(1)
 
     def yrows(k, start, size):
         return pl.ds(pl.multiple_of(mod(y + k, 4) * 64 + start, 8), size)
 
     def yterm(k, h, q):
-        return x_all.at[1, q, yrows(k, 32 * h, 32)]
+        return x_all.at[3 * c + q, yrows(k, 32 * h, 32)]
 
     yl = {}
     ys = {}
     for q in range(3):
-        px[q].wait_recv()
-        x_all[1, q] += x_in[q]
+        coupling_pair(q).wait_recv()
+        x_all[3 * c + q] += x_in[q]
         for d in range(2):
             yl[d, q] = copy(yterm(2, d, q), yin.at[d, q, 0], yto(sign[d]))
     for q in range(3):
@@ -229,7 +245,7 @@
             ys[d, q] = copy(yterm(sign[d], 1 - d, q), yin.at[d, q, 1], yto(sign[d]))
 
     fr = {}
-    for ky in (0, 2, 1, 3):
+    for ky in range(4):
         for d in range(2):
             fb[d, ky].wait_recv()
             part = zb_in[d, ky] + rpiece(2 * sign[d], ky)[...]
@@ -244,7 +260,7 @@
             yin[d, q, 0] += yterm(sign[d], d, q)[...]
             yl[d, q] = copy(yin.at[d, q, 0], yin.at[d, q, 2], yto(sign[d]))
 
-    for ky in (0, 2, 1, 3):
+    for ky in range(4):
         part = rpiece(0, ky)[...]
         for d in range(2):
             fc[d, ky].wait_recv()
@@ -346,23 +362,23 @@
     mh, ml = split(mbuf[...] + (m_in[1] + m_in[2] + m_in[3]))
     s = nt3(mh, ml, yh, yw)
     for i in range(16):
-        sbuf[i] = s[8 * i : 8 * i + 8, :]
+        sbuf[(i // 2) % 2, (i // 4) * 2 + i % 2] = s[8 * i : 8 * i + 8, :]
+    dp = copy(sbuf.at[1 - c], s_pair, core)
 
     e = lax.rem(y, 2)
 
-    def result(i, ry_, rc, rl):
-        to = {
-            "grp": y // 2, "rows_0": mod(y + ry_, 4), "rows_2": mod(c + rc, 2), "cols": mod(cl + rl, 2),
-        }
-        src = to["rows_0"] * 4 + to["rows_2"] * 2 + to["cols"]
+    def result(i, ry_, rl):
+        to = {"grp": y // 2, "rows_0": mod(y + ry_, 4), "cols": mod(cl + rl, 2)}
         return pltpu.make_async_remote_copy(
-            src_ref=sbuf.at[src], dst_ref=s_in.at[e, plane, c], send_sem=ssend.at[i],
-            recv_sem=srecv.at[e, plane, c], device_id=to, device_id_type=MESH,
+            src_ref=sbuf.at[c, to["rows_0"] * 2 + to["cols"]], dst_ref=s_in.at[e, plane],
+            send_sem=ssend.at[i], recv_sem=srecv.at[e, plane], device_id=to, device_id_type=MESH,
         )
 
-    results = [(a, b, d) for a in (0, 2, 1, 3) for b in range(2) for d in range(2)]
+    dp.wait_recv()
+    sbuf[c] += s_pair[...]
+    results = [(a, d) for a in (2, 1, 3, 0) for d in (1, 0)]
     for i, rel in enumerate(results):
-        if rel == (0, 0, 0):
+        if rel == (0, 0):
 
             @pl.when(y // 2 != g)
             def _(i=i, rel=rel):
@@ -370,25 +386,22 @@
 
             @pl.when(y // 2 == g)
             def _():
-                s_in[e, plane, c] = sbuf[y * 4 + c * 2 + cl]
+                s_in[e, plane] = sbuf[c, y * 2 + cl]
         else:
             result(i, *rel).start()
     for e_ in range(2):
         for j in range(4):
-            for cs in range(2):
-
-                def landed(e_=e_, j=j, cs=cs):
-                    pltpu.make_async_remote_copy(
-                        src_ref=sbuf.at[0], dst_ref=s_in.at[e_, j, cs], send_sem=ssend.at[0],
-                        recv_sem=srecv.at[e_, j, cs], device_id=core, device_id_type=MESH,
-                    ).wait_recv()
-
-                own = (e_ == e) & (j == plane) & (cs == c) & (y // 2 == g)
-                pl.when(jnp.logical_not(own))(landed)
+
+            def landed(e_=e_, j=j):
+                pltpu.make_async_remote_copy(
+                    src_ref=sbuf.at[0, 0], dst_ref=s_in.at[e_, j], send_sem=ssend.at[0],
+                    recv_sem=srecv.at[e_, j], device_id=core, device_id_type=MESH,
+                ).wait_recv()
+
+            own = (e_ == e) & (j == plane) & (y // 2 == g)
+            pl.when(jnp.logical_not(own))(landed)
     for e_ in range(2):
-        total = s_in[e_, 0, 0]
-        for n in range(1, 8):
-            total = total + s_in[e_, n // 2, n % 2]
+        total = s_in[e_, 0] + s_in[e_, 1] + (s_in[e_, 2] + s_in[e_, 3])
         out_ref[:, 256 * e_ : 256 * e_ + 256] = total * (1.0 / math.sqrt(1024))
 
     for i, (rel, e_) in enumerate(quarters):
@@ -400,13 +413,15 @@
         else:
             quarter(i, rel, e_).wait_send()
     for i, rel in enumerate(results):
-        if rel == (0, 0, 0):
+        if rel == (0, 0):
 
             @pl.when(y // 2 != g)
             def _(i=i, rel=rel):
                 result(i, *rel).wait_send()
         else:
             result(i, *rel).wait_send()
+    for t in range(3):
+        coupling_pair(t).wait_send()
     for d in started:
         d.wait_send()
 
@@ -433,7 +448,7 @@
             pltpu.VMEM((1536, 128), F32),
             pltpu.VMEM((1536, 128), F32),
             pltpu.VMEM((1536, 128), F32),
-            pltpu.VMEM((2, 3, 256, 256), F32),
+            pltpu.VMEM((6, 256, 256), F32),
             pltpu.VMEM((3, 256, 256), F32),
             pltpu.VMEM((2, 2, 48, 128), F32),
             pltpu.VMEM((2, 4, 48, 128), F32),
@@ -452,15 +467,18 @@
             pltpu.VMEM((8, 32, 128), F32),
             pltpu.VMEM((128, 128), F32),
             pltpu.VMEM((4, 128, 128), F32),
-            pltpu.VMEM((16, 8, 256), F32),
-            pltpu.VMEM((2, 4, 2, 8, 256), F32),
+            pltpu.VMEM((2, 8, 8, 256), F32),
+            pltpu.VMEM((8, 8, 256), F32),
+            pltpu.VMEM((2, 4, 8, 256), F32),
             pltpu.SemaphoreType.DMA((NK,)),
             pltpu.SemaphoreType.DMA((6,)),
             pltpu.SemaphoreType.DMA((6,)),
+            pltpu.SemaphoreType.DMA((3,)),
+            pltpu.SemaphoreType.DMA((3,)),
             pltpu.SemaphoreType.DMA((16,)),
             pltpu.SemaphoreType.DMA((4, 4)),
-            pltpu.SemaphoreType.DMA((16,)),
-            pltpu.SemaphoreType.DMA((2, 4, 2)),
+            pltpu.SemaphoreType.DMA((8,)),
+            pltpu.SemaphoreType.DMA((2, 4)),
             pltpu.SemaphoreType.DMA((112,)),
             pltpu.SemaphoreType.DMA((112,)),
         ],

time: 61.6 us -> 59.1 us (0.959)
  Pallas kernels: 60.1 us -> 57.6 us
    pallas_call x1, Pallas kernels: 60.1 us -> 57.6 us  [per_device(): pl.pallas_call(window_kernel, out_shape=jax.ShapeDtypeStruct((8, 512), F3...]
where the time goes in v6:
time: 59.1 us; the launch traced here: 58.9 us
  Pallas kernels  57.6 us (97%)
  local copies, waits for them, and re-layouts  1.32 us (2%)
    pallas_call x1, Pallas kernels, per_device(): pl.pallas_call(window_kernel, out_shape=jax.ShapeDtypeStruct((8, 512), F3...  57.6 us
    unnamed x1, local copies, waits for them, and re-layouts  1.32 us

profile of v6, /device:TPU:1, one launch (start us, length us, event | category | flops | bytes accessed | tf_op | source)
XLA Modules:
  0.0 58.9 jit_solution(4921384146010813257)
XLA Ops:
  0.0 57.6 %window.1 = f32[8,512]{1,0:T(8,128)} custom-call(s32[1536]{0:T(1024)} %occ.1, s32[1536]{0:T(1024)} %vir.1, s32[1024]{0:T(1024)} %fidx.1, f32[16]{0:T(128)} %ftab.1, f32[1536]{0:T(1024)} %weight.1, f32[768]{0:T(1024)} %coulomb.1, f32[768,1024]{1,0:T(8,128)} %v_hbm.1), custom_call_target="tpu_custom_call" | custom-call | tf_op jit(solution)/shard_map/window/pallas_call | solution.py:432
  57.6 1.3 %copy.9 = f32[8,512]{1,0:T(8,128)} copy(f32[8,512]{1,0:T(8,128)} %window.1) | data formatting | bytes 32768

commit v7 on v6

--- a/solution.py
+++ b/solution.py
@@ -47,8 +47,8 @@
 
 
 def window_kernel(
-    occ, vir, fidx, ftab, weight, coulomb, v_hbm, out_ref,
-    v_ref, vt, pt, qt, ph, pw, qh, ql, nh, nl,
+    occ_hbm, vir_hbm, fidx_hbm, ftab_hbm, weight_hbm, coulomb_hbm, v_hbm, out_ref,
+    occ, vir, fidx, ftab, weight, coulomb, v_ref, vt, pt, qt, ph, pw, qh, ql, nh, nl,
     r_own, r_oth, r_in, x_all, x_in,
     za_in, zb_in, zc_in, zr_in, yin, rfin, xfin, ry_in, xz_in,
     rq, xt, yt, xq, y32, yq, mbuf, m_in, sbuf, s_pair, s_in,
@@ -92,7 +92,14 @@
     for k in range(NK):
         rows = pl.ds(k * 128, 128)
         loads.append(pltpu.make_async_copy(v_hbm.at[rows], v_ref.at[rows], load.at[k]))
-        loads[k].start()
+    smalls = (
+        (occ_hbm, occ), (vir_hbm, vir), (weight_hbm, weight),
+        (coulomb_hbm, coulomb), (fidx_hbm, fidx), (ftab_hbm, ftab),
+    )
+    for k, (src, dst) in enumerate(smalls):
+        loads.append(pltpu.make_async_copy(src, dst, load.at[NK + k]))
+    for d in loads:
+        d.start()
 
     barrier = pltpu.get_barrier_semaphore()
     for k in range(1, 8):
@@ -105,6 +112,9 @@
         for nb in range(8):
             block = v_ref[k * 128 : (k + 1) * 128, nb * 128 : (nb + 1) * 128]
             vt2[pl.ds(nb * 1024 + k, 128, stride=8), :] = block.T
+
+    for d in loads[NK:]:
+        d.wait()
 
     def gather_some(base, to, count, rows=pt):
         for u in range(count):
@@ -245,7 +255,9 @@
             ys[d, q] = copy(yterm(sign[d], 1 - d, q), yin.at[d, q, 1], yto(sign[d]))
 
     fr = {}
-    for ky in range(4):
+    xz = []
+
+    def relay(ky):
         for d in range(2):
             fb[d, ky].wait_recv()
             part = zb_in[d, ky] + rpiece(2 * sign[d], ky)[...]
@@ -254,23 +266,22 @@
                 part = part + za_in[d, ky % 2]
             zb_in[d, ky] = part
             fr[d, ky] = copy(zb_in.at[d, ky], zr_in.at[d, ky], zto(2 * sign[d]))
-    for q in range(3):
+
+    def pass_on(q):
         for d in range(2):
             yl[d, q].wait_recv()
             yin[d, q, 0] += yterm(sign[d], d, q)[...]
             yl[d, q] = copy(yin.at[d, q, 0], yin.at[d, q, 2], yto(sign[d]))
 
-    for ky in range(4):
+    def finish_piece(ky):
         part = rpiece(0, ky)[...]
         for d in range(2):
             fc[d, ky].wait_recv()
             fr[d, ky].wait_recv()
             part = part + (zc_in[d, ky] + zr_in[d, ky])
         rfin[ky] = part
-    ry = [copy(rfin.at[mod(y + k, 4)], ry_in.at[k], yto(k)) for k in (2, 1, 3)]
-
-    xz = []
-    for q in range(3):
+
+    def finish_rows(q):
         for d in range(2):
             ys[d, q].wait_recv()
             yl[d, q].wait_recv()
@@ -281,6 +292,22 @@
         for k in (4, 3, 5, 2, 6, 1, 7):
             rows = pl.ds(pl.multiple_of(mod(z + k, 8) * 8, 8), 8)
             xz.append(copy(xfin.at[q, rows], xz_in.at[k, q], zto(k)))
+
+    relay(0)
+    relay(1)
+    pass_on(0)
+    relay(2)
+    pass_on(1)
+    relay(3)
+    pass_on(2)
+    finish_piece(0)
+    finish_piece(1)
+    finish_rows(0)
+    finish_rows(1)
+    finish_piece(2)
+    finish_rows(2)
+    finish_piece(3)
+    ry = [copy(rfin.at[mod(y + k, 4)], ry_in.at[k], yto(k)) for k in (2, 1, 3)]
 
     for d in ry:
         d.wait_recv()
@@ -427,14 +454,19 @@
 
 
 def per_device(band_vectors, coulomb, pair_weight, occ_index, vir_index, freq_index, freq_table):
-    smem = pl.BlockSpec(memory_space=pltpu.SMEM)
     vmem = pl.BlockSpec(memory_space=pltpu.VMEM)
     return pl.pallas_call(
         window_kernel,
         out_shape=jax.ShapeDtypeStruct((8, 512), F32),
-        in_specs=[smem, smem, smem, smem, vmem, vmem, pl.BlockSpec(memory_space=pl.ANY)],
+        in_specs=[pl.BlockSpec(memory_space=pl.ANY)] * 7,
         out_specs=vmem,
         scratch_shapes=[
+            pltpu.SMEM((1536,), jnp.int32),
+            pltpu.SMEM((1536,), jnp.int32),
+            pltpu.SMEM((1024,), jnp.int32),
+            pltpu.SMEM((16,), F32),
+            pltpu.VMEM((1536,), F32),
+            pltpu.VMEM((KB,), F32),
             pltpu.VMEM((KB, 1024), F32),
             pltpu.VMEM((1024, 8, 128), F32),
             pltpu.VMEM((256, 8, 128), F32),
@@ -470,7 +502,7 @@
             pltpu.VMEM((2, 8, 8, 256), F32),
             pltpu.VMEM((8, 8, 256), F32),
             pltpu.VMEM((2, 4, 8, 256), F32),
-            pltpu.SemaphoreType.DMA((NK,)),
+            pltpu.SemaphoreType.DMA((NK + 6,)),
             pltpu.SemaphoreType.DMA((6,)),
             pltpu.SemaphoreType.DMA((6,)),
             pltpu.SemaphoreType.DMA((3,)),

time: 59.1 us -> 55.7 us (0.942)
  Pallas kernels: 57.6 us -> 54.1 us
    pallas_call x1, Pallas kernels: 57.6 us -> 54.1 us  [per_device(): pl.pallas_call(window_kernel, out_shape=jax.ShapeDtypeStruct((8, 512), F3...]
where the time goes in v7:
time: 55.7 us; the launch traced here: 55.5 us
  Pallas kernels  54.1 us (97%)
  local copies, waits for them, and re-layouts  1.32 us (2%)
    pallas_call x1, Pallas kernels, per_device(): pl.pallas_call(window_kernel, out_shape=jax.ShapeDtypeStruct((8, 512), F3...  54.1 us
    unnamed x1, local copies, waits for them, and re-layouts  1.32 us

profile of v7, /device:TPU:1, one launch (start us, length us, event | category | flops | bytes accessed | tf_op | source)
XLA Modules:
  0.0 55.5 jit_solution(10075533453909844329)
XLA Ops:
  0.0 54.1 %window.1 = f32[8,512]{1,0:T(8,128)} custom-call(s32[1536]{0:T(1024)} %occ_hbm.1, s32[1536]{0:T(1024)} %vir_hbm.1, s32[1024]{0:T(1024)} %fidx_hbm.1, f32[16]{0:T(128)} %ftab_hbm.1, f32[1536]{0:T(1024)} %weight_hbm.1, f32[768]{0:T(1024)} %coulomb_hbm.1, f32[768,1024]{1,0:T(8,128)} %v_hbm.1), custom_call_target="tpu_custom_call" | custom-call | tf_op jit(solution)/shard_map/window/pallas_call | solution.py:458
  54.2 1.3 %copy.9 = f32[8,512]{1,0:T(8,128)} copy(f32[8,512]{1,0:T(8,128)} %window.1) | data formatting | bytes 32768

commit v8 on v7

--- a/solution.py
+++ b/solution.py
@@ -120,13 +120,6 @@
         for u in range(count):
             rows[to + u] = vt[occ[base + u]] * vt[vir[base + u]]
 
-    def gather(base, to):
-        def some(i, carry):
-            gather_some(base + i * 32, to + i * 32, 32)
-            return carry
-
-        lax.fori_loop(0, 4, some, 0)
-
     def weights(base):
         row = weight[pl.ds(pl.multiple_of(base, 128), 128)].reshape(1, 128)
         return jnp.broadcast_to(row, (128, 128)).T
@@ -135,14 +128,12 @@
         return coulomb[k * 128 : (k + 1) * 128].reshape(1, 128)
 
     window = [256 * plane + 128 * mod(c + s, 2) for s in range(2)]
-    for s in range(2):
-        gather(window[s], 128 * s)
 
     def window_rows():
         for s in range(2):
             w = weights(window[s])
             for k in range(NK):
-                x = pt2s[0][pl.ds(s * 1024 + k, 128, stride=8), :] * w * cvec(k)
+                x = pt2s[1][pl.ds(s * 1024 + k, 128, stride=8), :] * w * cvec(k)
                 hi, lo = split(x)
                 qh[s * 128 : (s + 1) * 128, k * 128 : (k + 1) * 128] = hi
                 ql[s * 128 : (s + 1) * 128, k * 128 : (k + 1) * 128] = lo
@@ -169,11 +160,14 @@
     def place(i):
         return [512 * (i % 3) + 256 * s + 128 * (i // 3) for s in range(2)]
 
+    def buffer_of(i):
+        return 0 if i == 0 else (i + 1) % 2
+
     def rows_of(i, bases):
         for s in range(2):
             w = weights(bases[s])
             for k in range(NK):
-                hi, lo = split(pt2s[(i + 1) % 2][pl.ds(s * 1024 + k, 128, stride=8), :] * w)
+                hi, lo = split(pt2s[buffer_of(i)][pl.ds(s * 1024 + k, 128, stride=8), :] * w)
                 ph[i, s * 128 : (s + 1) * 128, k * 128 : (k + 1) * 128] = hi
                 pw[i, s * 128 : (s + 1) * 128, k * 128 : (k + 1) * 128] = lo
 
@@ -191,20 +185,17 @@
     fb = {}
     fc = {}
 
-    def start_sums(half):
-        for i in range(3):
-            to_partner(3 * half + i).wait()
-        rows = slice(768 * half, 768 * half + 768)
+    def start_sum(ky):
+        for i in ((0, 1), (2,), (3, 4), (5,))[ky]:
+            to_partner(i).wait()
+        rows = slice(384 * ky, 384 * ky + 384)
         r_own[rows] += r_in[rows]
-        for j in range(2):
-            ky = 2 * half + j
-            fa[half, j] = copy(rpiece(4 * sign[half], ky), za_in.at[half, j], zto(2 * sign[half]))
-        for ky in (2 * half, 2 * half + 1):
-            for d in range(2):
-                fb[d, ky] = copy(rpiece(3 * sign[d], ky), zb_in.at[d, ky], zto(sign[d]))
-        for ky in (2 * half, 2 * half + 1):
-            for d in range(2):
-                fc[d, ky] = copy(rpiece(sign[d], ky), zc_in.at[d, ky], zto(sign[d]))
+        n, j = ky // 2, ky % 2
+        fa[n, j] = copy(rpiece(4 * sign[n], ky), za_in.at[n, j], zto(2 * sign[n]))
+        for d in range(2):
+            fb[d, ky] = copy(rpiece(3 * sign[d], ky), zb_in.at[d, ky], zto(sign[d]))
+        for d in range(2):
+            fc[d, ky] = copy(rpiece(sign[d], ky), zc_in.at[d, ky], zto(sign[d]))
 
     def coupling_pair(i):
         return pltpu.make_async_remote_copy(
@@ -212,30 +203,48 @@
             recv_sem=xprecv.at[i % 3], device_id=core, device_id_type=MESH,
         )
 
-    for i in range(8):
-        if i == 2:
-            pl.semaphore_wait(barrier, 38)
-        if i < 6:
-            for e in range(2):
-                gather_some(place(i)[e], 128 * e, 128, pts[(i + 1) % 2])
-        if i == 0:
-            window_rows()
-        if i == 1:
-            band_rows()
-        if 1 <= i < 7:
-            rows_of(i - 1, place(i - 1))
-        if i >= 2:
-            n = i - 2
-            response_of(n)
-            x_all[n] = nt3(nh[...], nl[...], ph[n], pw[n])
-            to_partner(n).start()
-
-            @pl.when(c != n // 3)
-            def _(n=n):
-                coupling_pair(n).start()
-        if i == 5:
-            start_sums(0)
-    start_sums(1)
+    def gather_block(i):
+        for e in range(2):
+            gather_some(place(i)[e], 128 * e, 128, pts[buffer_of(i)])
+
+    def coupling_of(n):
+        x_all[n] = nt3(nh[...], nl[...], ph[n], pw[n])
+
+    def send_coupling(n):
+        @pl.when(c != n // 3)
+        def _():
+            coupling_pair(n).start()
+
+    gather_block(0)
+    band_rows()
+    for e in range(2):
+        gather_some(window[e], 128 * e, 128, pts[1])
+    rows_of(0, place(0))
+    gather_block(1)
+    window_rows()
+    coupling_of(0)
+    pl.semaphore_wait(barrier, 38)
+    send_coupling(0)
+    gather_block(2)
+    rows_of(1, place(1))
+    response_of(0)
+    to_partner(0).start()
+    for n in range(1, 5):
+        if n + 2 < 6:
+            gather_block(n + 2)
+        rows_of(n + 1, place(n + 1))
+        response_of(n)
+        coupling_of(n)
+        to_partner(n).start()
+        send_coupling(n)
+        if n in (2, 3):
+            start_sum(n - 2)
+    response_of(5)
+    to_partner(5).start()
+    start_sum(2)
+    coupling_of(5)
+    send_coupling(5)
+    start_sum(3)
 
     def yrows(k, start, size):
         return pl.ds(pl.multiple_of(mod(y + k, 4) * 64 + start, 8), size)

time: 55.7 us -> 54.2 us (0.973)
  Pallas kernels: 54.1 us -> 52.6 us
    pallas_call x1, Pallas kernels: 54.1 us -> 52.6 us  [per_device(): pl.pallas_call(window_kernel, out_shape=jax.ShapeDtypeStruct((8, 512), F3...]
where the time goes in v8:
time: 54.2 us; the launch traced here: 53.9 us
  Pallas kernels  52.6 us (97%)
  local copies, waits for them, and re-layouts  1.32 us (2%)
    pallas_call x1, Pallas kernels, per_device(): pl.pallas_call(window_kernel, out_shape=jax.ShapeDtypeStruct((8, 512), F3...  52.6 us
    unnamed x1, local copies, waits for them, and re-layouts  1.32 us

profile of v8, /device:TPU:1, one launch (start us, length us, event | category | flops | bytes accessed | tf_op | source)
XLA Modules:
  0.0 53.9 jit_solution(2880825479874203942)
XLA Ops:
  0.0 52.6 %window.1 = f32[8,512]{1,0:T(8,128)} custom-call(s32[1536]{0:T(1024)} %occ_hbm.1, s32[1536]{0:T(1024)} %vir_hbm.1, s32[1024]{0:T(1024)} %fidx_hbm.1, f32[16]{0:T(128)} %ftab_hbm.1, f32[1536]{0:T(1024)} %weight_hbm.1, f32[768]{0:T(1024)} %coulomb_hbm.1, f32[768,1024]{1,0:T(8,128)} %v_hbm.1), custom_call_target="tpu_custom_call" | custom-call | tf_op jit(solution)/shard_map/window/pallas_call | solution.py:467
  52.6 1.3 %copy.9 = f32[8,512]{1,0:T(8,128)} copy(f32[8,512]{1,0:T(8,128)} %window.1) | data formatting | bytes 32768

commit v9 on v8

--- a/solution.py
+++ b/solution.py
@@ -202,6 +202,23 @@
             src_ref=x_all.at[i], dst_ref=x_in.at[i % 3], send_sem=xpsend.at[i % 3],
             recv_sem=xprecv.at[i % 3], device_id=core, device_id_type=MESH,
         )
+
+    def yterm(k, h, q):
+        rows = pl.multiple_of(mod(y + k, 4) * 64 + 32 * h, 8)
+        return x_all.at[3 * c + q, pl.ds(rows, 32)]
+
+    yl = {}
+    ys = {}
+
+    def start_long(q):
+        coupling_pair(q).wait_recv()
+        x_all[3 * c + q] += x_in[q]
+        for d in range(2):
+            yl[d, q] = copy(yterm(2, d, q), yin.at[d, q, 0], yto(sign[d]))
+
+    def start_short(q):
+        for d in range(2):
+            ys[d, q] = copy(yterm(sign[d], 1 - d, q), yin.at[d, q, 1], yto(sign[d]))
 
     def gather_block(i):
         for e in range(2):
@@ -241,27 +258,16 @@
             start_sum(n - 2)
     response_of(5)
     to_partner(5).start()
+    start_long(0)
+    start_short(0)
     start_sum(2)
     coupling_of(5)
     send_coupling(5)
+    start_long(1)
     start_sum(3)
-
-    def yrows(k, start, size):
-        return pl.ds(pl.multiple_of(mod(y + k, 4) * 64 + start, 8), size)
-
-    def yterm(k, h, q):
-        return x_all.at[3 * c + q, yrows(k, 32 * h, 32)]
-
-    yl = {}
-    ys = {}
-    for q in range(3):
-        coupling_pair(q).wait_recv()
-        x_all[3 * c + q] += x_in[q]
-        for d in range(2):
-            yl[d, q] = copy(yterm(2, d, q), yin.at[d, q, 0], yto(sign[d]))
-    for q in range(3):
-        for d in range(2):
-            ys[d, q] = copy(yterm(sign[d], 1 - d, q), yin.at[d, q, 1], yto(sign[d]))
+    start_long(2)
+    start_short(1)
+    start_short(2)
 
     fr = {}
     xz = []
@@ -303,8 +309,8 @@
             xz.append(copy(xfin.at[q, rows], xz_in.at[k, q], zto(k)))
 
     relay(0)
+    pass_on(0)
     relay(1)
-    pass_on(0)
     relay(2)
     pass_on(1)
     relay(3)

time: 54.2 us -> 54.6 us (level)
    pallas_call x1, Pallas kernels: 52.6 us -> 53.1 us  [per_device(): pl.pallas_call(window_kernel, out_shape=jax.ShapeDtypeStruct((8, 512), F3...]
where the time goes in v9:
time: 54.6 us; the launch traced here: 54.5 us
  Pallas kernels  53.1 us (97%)
  local copies, waits for them, and re-layouts  1.32 us (2%)
    pallas_call x1, Pallas kernels, per_device(): pl.pallas_call(window_kernel, out_shape=jax.ShapeDtypeStruct((8, 512), F3...  53.1 us
    unnamed x1, local copies, waits for them, and re-layouts  1.32 us

profile of v9, /device:TPU:1, one launch (start us, length us, event | category | flops | bytes accessed | tf_op | source)
XLA Modules:
  0.0 54.5 jit_solution(4403979291902051602)
XLA Ops:
  0.0 53.1 %window.1 = f32[8,512]{1,0:T(8,128)} custom-call(s32[1536]{0:T(1024)} %occ_hbm.1, s32[1536]{0:T(1024)} %vir_hbm.1, s32[1024]{0:T(1024)} %fidx_hbm.1, f32[16]{0:T(128)} %ftab_hbm.1, f32[1536]{0:T(1024)} %weight_hbm.1, f32[768]{0:T(1024)} %coulomb_hbm.1, f32[768,1024]{1,0:T(8,128)} %v_hbm.1), custom_call_target="tpu_custom_call" | custom-call | tf_op jit(solution)/shard_map/window/pallas_call | solution.py:473
  53.1 1.3 %copy.9 = f32[8,512]{1,0:T(8,128)} copy(f32[8,512]{1,0:T(8,128)} %window.1) | data formatting | bytes 32768

commit v10 on v8

--- a/solution.py
+++ b/solution.py
@@ -314,9 +314,9 @@
     finish_rows(0)
     finish_rows(1)
     finish_piece(2)
-    finish_rows(2)
     finish_piece(3)
     ry = [copy(rfin.at[mod(y + k, 4)], ry_in.at[k], yto(k)) for k in (2, 1, 3)]
+    finish_rows(2)
 
     for d in ry:
         d.wait_recv()

time: 54.2 us -> 54.9 us (1.013)
  Pallas kernels: 52.6 us -> 53.5 us
    pallas_call x1, Pallas kernels: 52.6 us -> 53.5 us  [per_device(): pl.pallas_call(window_kernel, out_shape=jax.ShapeDtypeStruct((8, 512), F3...]
where the time goes in v10:
time: 54.9 us; the launch traced here: 54.8 us
  Pallas kernels  53.5 us (97%)
  local copies, waits for them, and re-layouts  1.32 us (2%)
    pallas_call x1, Pallas kernels, per_device(): pl.pallas_call(window_kernel, out_shape=jax.ShapeDtypeStruct((8, 512), F3...  53.5 us
    unnamed x1, local copies, waits for them, and re-layouts  1.32 us

profile of v10, /device:TPU:1, one launch (start us, length us, event | category | flops | bytes accessed | tf_op | source)
XLA Modules:
  0.0 54.8 jit_solution(13876603237274853085)
XLA Ops:
  0.0 53.5 %window.1 = f32[8,512]{1,0:T(8,128)} custom-call(s32[1536]{0:T(1024)} %occ_hbm.1, s32[1536]{0:T(1024)} %vir_hbm.1, s32[1024]{0:T(1024)} %fidx_hbm.1, f32[16]{0:T(128)} %ftab_hbm.1, f32[1536]{0:T(1024)} %weight_hbm.1, f32[768]{0:T(1024)} %coulomb_hbm.1, f32[768,1024]{1,0:T(8,128)} %v_hbm.1), custom_call_target="tpu_custom_call" | custom-call | tf_op jit(solution)/shard_map/window/pallas_call | solution.py:467
  53.5 1.3 %copy.9 = f32[8,512]{1,0:T(8,128)} copy(f32[8,512]{1,0:T(8,128)} %window.1) | data formatting | bytes 32768
